TPU v7x, 32 devices: a whole 2x2x4 slice. The times are simulated.
32 devices in a mesh: row: 4 (over y, core), col: 8 (over z, x).
Axes of the slice: x: 2, y: 2, z: 4, core: 2. Of those that a mesh axis runs over, the one named last changes fastest.
Arguments:
- spectra: float32 [2, 16, 1024, 512], P(None, None, ('col', 'row')), as said below
- pair_mask: int32 [4, 8], P('row', 'col'), may hold values 0 or 1
- band_range: int32 [2], replicated, may hold values from 0 to 512, as said below
Outputs:
- correlations: bfloat16 [1024, 1024, 201], P('row', 'col')
Inputs may be any that keep to these rules, and one draw needn't show every extreme that they name: `spectra`: every channel's spectrum carries its own amplitude. band_range[0] < band_range[1].
All inputs are finite; a program needn't handle non-finite values. No bound on the sum of `pair_mask` on one device may be relied on, other than what follows from the above.
Results may differ from a plain program's by a relative error of at most 0.0061.
Values may be sent and summed in bfloat16 or wider, within the bound.
No kernel may reach another device: no remote copies, remote signals or barrier semaphores. Data moves between devices by JAX's collectives and lax.ppermute only.
A program may use at most 320 MiB of HBM per device.

v0:
```python
import functools
import math

import jax
import jax.numpy as jnp
from jax import lax
from jax.experimental import pallas as pl
from jax.experimental.pallas import tpu as pltpu
from jax.sharding import Mesh
from jax.sharding import PartitionSpec as P

W = 16
FB = 512
LAGS = 201
NFFT = 15000
F0 = 60
EPS = 1e-06

SEGMENTS = 4
ROWS = FB // SEGMENTS
PAIRS = ROWS // 2
LAG_PAD = 208


def whiten_kernel(*refs, width, parts):
    x_refs, whole_ref, out_refs, scratch = refs[:SEGMENTS], refs[SEGMENTS], refs[SEGMENTS + 1 : -1], refs[-1]

    def channel(c, carry):
        tiles = [x_ref[pl.ds(c, 2 * W, stride=width), :] for x_ref in x_refs]
        total = sum(v[:W] * v[:W] + v[W:] * v[W:] for v in tiles)
        power = jnp.sum(total, axis=-1, keepdims=True) * (1.0 / FB)
        scale = lax.rsqrt(power + EPS)
        scale = jnp.concatenate([scale, scale], axis=0)
        stacked = jnp.concatenate([v * scale for v in tiles], axis=0)
        scratch[pl.ds(c, ROWS, stride=width), :] = stacked.T
        return carry

    lax.fori_loop(0, width, channel, 0, unroll=2)
    step = width // parts
    full = scratch[...].reshape(ROWS, width, 128).astype(jnp.bfloat16)
    whole_ref[...] = full
    for g, out_ref in enumerate(out_refs):
        out_ref[...] = full[:, g * step : (g + 1) * step, :]


def whiten(spectra, parts):
    width = spectra.shape[2]
    widths = [width] + ([width // parts] * parts if parts > 1 else [])
    lines = 2 * W * width
    flat = spectra.reshape(lines, FB)
    return pl.pallas_call(
        functools.partial(whiten_kernel, width=width, parts=parts),
        out_shape=[jax.ShapeDtypeStruct((ROWS, n, 128), jnp.bfloat16) for n in widths],
        grid=(1,),
        in_specs=[pl.BlockSpec((lines, ROWS), functools.partial(lambda q, i: (0, q), q)) for q in range(SEGMENTS)],
        out_specs=[pl.BlockSpec((ROWS, n, 128), lambda i: (0, 0, 0)) for n in widths],
        scratch_shapes=[pltpu.VMEM((ROWS * width, 128), jnp.float32)],
        compiler_params=pltpu.CompilerParams(vmem_limit_bytes=40 << 20),
        name="whiten",
    )(*[flat] * SEGMENTS)


def weights_kernel(offset_ref, *refs, count, step):
    in_refs, out_ref, clear_ref, scratch = refs[:count], refs[count], refs[count + 1], refs[count + 2]
    clear_ref[...] = jnp.zeros_like(clear_ref)
    for i in range(count):
        at = pl.multiple_of(offset_ref[i], step)
        scratch[:, pl.ds(at, step), :] = in_refs[i][...].astype(jnp.float32)

    def row(t, carry):
        for s in range(2):
            real = scratch[2 * t + s].T
            pieces = []
            for q in range(SEGMENTS):
                lo = q * 2 * W
                pieces += [-real[lo + W : lo + 2 * W], real[lo : lo + W]]
            imag = jnp.concatenate(pieces, axis=0)
            both = jnp.concatenate([real, imag], axis=1).astype(jnp.bfloat16)
            out_ref[t, s * 128 : (s + 1) * 128, :] = both
        return carry

    lax.fori_loop(0, out_ref.shape[0], row, 0, unroll=2)


def weights(offsets, shards, height):
    count = len(shards)
    step = shards[0].shape[1]
    tiles = 4
    return pl.pallas_call(
        functools.partial(weights_kernel, count=count, step=step),
        out_shape=[
            jax.ShapeDtypeStruct((PAIRS, 256, 256), jnp.bfloat16),
            jax.ShapeDtypeStruct((LAGS, height, count * step), jnp.bfloat16),
        ],
        grid_spec=pltpu.PrefetchScalarGridSpec(
            num_scalar_prefetch=1,
            grid=(tiles,),
            in_specs=[pl.BlockSpec((ROWS // tiles, step, 128), lambda i, o: (i, 0, 0))] * count,
            out_specs=[
                pl.BlockSpec((PAIRS // tiles, 256, 256), lambda i, o: (i, 0, 0)),
                pl.BlockSpec((LAGS, height // tiles, count * step), lambda i, o: (0, i, 0)),
            ],
            scratch_shapes=[pltpu.VMEM((ROWS // tiles, count * step, 128), jnp.float32)],
        ),
        compiler_params=pltpu.CompilerParams(vmem_limit_bytes=40 << 20),
        name="weights",
    )(offsets, *shards)


def pair_kernel(meta_ref, *refs, count, height, unroll_sum, unroll_lag, pitch):
    x_refs = refs[:count]
    w_ref, t_ref, _, out_ref = refs[count : count + 4]
    xbuf, wide, wbuf, tbuf, cross, lags, stage, sems = refs[count + 4 :]

    @pl.when(meta_ref[0] >= 0)
    def _():
        for i in range(count):

            @pl.when(meta_ref[0] == i)
            def _(i=i):
                pltpu.make_async_copy(x_refs[i], xbuf, sems.at[0]).start()

        others = [
            pltpu.make_async_copy(w_ref, wbuf, sems.at[1]),
            pltpu.make_async_copy(t_ref, tbuf, sems.at[2]),
        ]
        for copy in others:
            copy.start()
        pltpu.make_async_copy(x_refs[0], xbuf, sems.at[0]).wait()
        wide[...] = xbuf[...].astype(jnp.float32).reshape(ROWS * height, 128)
        for copy in others:
            copy.wait()

        sub = lax.broadcasted_iota(jnp.int32, (8, 128), 0)
        segment = lax.broadcasted_iota(jnp.int32, (8, 128), 1) // (2 * W)
        masks = (segment == sub, segment == sub - SEGMENTS)

        def window_sums(h, carry):
            halves = []
            for u in range(2):
                pair = 2 * h + u
                rows = []
                for a in range(height):
                    halves_of_k = [
                        jnp.where(masks[s], wide[pl.ds((2 * pair + s) * height + a, 8, stride=0), :], 0.0)
                        for s in range(2)
                    ]
                    rows.append(jnp.concatenate(halves_of_k, axis=1))
                left = jnp.concatenate(rows, axis=0).astype(jnp.bfloat16)
                sums = jnp.dot(left, wbuf[pair], preferred_element_type=jnp.float32)
                halves.append(sums.reshape(height, 8, 256))
            both = jnp.concatenate(halves, axis=1).astype(jnp.bfloat16)
            cross[:, pl.ds(pl.multiple_of(h * 16, 16), 16), :] = both
            return carry

        lax.fori_loop(0, PAIRS // 2, window_sums, 0, unroll=unroll_sum)

        def lag_sums(h, carry):
            first, second = cross[2 * h], cross[2 * h + 1]
            real = jnp.concatenate([first[:, :128], second[:, :128]], axis=1)
            imag = jnp.concatenate([first[:, 128:], second[:, 128:]], axis=1)
            right = jnp.concatenate([real, imag], axis=0)
            out = jnp.dot(tbuf[...], right, preferred_element_type=jnp.float32)
            out = out * (1.0 / math.sqrt(W * FB))
            lags[pl.ds(2 * h, LAG_PAD, stride=pitch), :] = out[:, :128]
            lags[pl.ds(2 * h + 1, LAG_PAD, stride=pitch), :] = out[:, 128:]
            return carry

        lax.fori_loop(0, height // 2, lag_sums, 0, unroll=unroll_lag)
        stage[...] = lags[...].reshape(LAG_PAD, pitch, 128)[:LAGS, :height].astype(jnp.bfloat16)
        at = pl.multiple_of(meta_ref[1], height)
        back = pltpu.make_async_copy(stage, out_ref.at[:, pl.ds(at, height), :], sems.at[0])
        back.start()
        back.wait()


def pair_block(choice, place, shards, right, table, out, unroll_sum=8, unroll_lag=8, pad=8):
    count = len(shards)
    height = shards[0].shape[1]
    meta = jnp.stack([choice, place]).astype(jnp.int32)
    anywhere = pl.BlockSpec(memory_space=pl.ANY)
    return pl.pallas_call(
        functools.partial(
            pair_kernel,
            count=count,
            height=height,
            unroll_sum=unroll_sum,
            unroll_lag=unroll_lag,
            pitch=height + pad,
        ),
        out_shape=jax.ShapeDtypeStruct(out.shape, out.dtype),
        grid_spec=pltpu.PrefetchScalarGridSpec(
            num_scalar_prefetch=1,
            grid=(),
            in_specs=[anywhere] * (count + 3),
            out_specs=anywhere,
            scratch_shapes=[
                pltpu.VMEM((ROWS, height, 128), jnp.bfloat16),
                pltpu.VMEM((ROWS * height, 128), jnp.float32),
                pltpu.VMEM((PAIRS, 256, 256), jnp.bfloat16),
                pltpu.VMEM((LAG_PAD, 2 * FB), jnp.bfloat16),
                pltpu.VMEM((height, FB, 256), jnp.bfloat16),
                pltpu.VMEM((LAG_PAD * (height + pad), 128), jnp.float32),
                pltpu.VMEM((LAGS, height, 128), jnp.bfloat16),
                pltpu.SemaphoreType.DMA((3,)),
            ],
        ),
        input_output_aliases={count + 3: 0},
        compiler_params=pltpu.CompilerParams(vmem_limit_bytes=60 << 20),
        cost_estimate=pl.CostEstimate(
            flops=2 * height * FB * 256 * 8 * 32 + 2 * height * 128 * 2 * FB * LAG_PAD,
            bytes_accessed=PAIRS * 256 * 256 * 2 + 2 * height * 128 * LAGS,
            transcendentals=0,
        ),
        name="pair_block",
    )(meta, *shards, right, table, out)


def make_table(band_range):
    order = jnp.arange(FB, dtype=jnp.int32)
    freq_index = (order % SEGMENTS) * ROWS + order // SEGMENTS
    lag_index = jnp.arange(LAG_PAD, dtype=jnp.int32) - LAGS // 2
    turns = jnp.mod((F0 + freq_index)[None, :] * lag_index[:, None], NFFT)
    theta = turns.astype(jnp.float32) * (2.0 * math.pi / NFFT)
    inband = ((freq_index >= band_range[0]) & (freq_index < band_range[1])).astype(jnp.float32)[None, :]
    return jnp.concatenate([inband * jnp.cos(theta), -inband * jnp.sin(theta)], axis=1).astype(jnp.bfloat16)


def relay_body(spectra, request, table):
    rows, sides = lax.axis_size("row"), lax.axis_size("side")
    axes = ("row", "plane", "side")
    row_id, plane, side = (lax.axis_index(name) for name in axes)
    width = spectra.shape[2]
    core, chip = row_id % 2, row_id // 2
    depth = plane - row_id
    devices = [(r, p, x) for r in range(rows) for p in range(rows) for x in range(sides)]

    def send(value, pairs):
        number = [tuple((r * rows + p) * sides + x for r, p, x in pair) for pair in pairs]
        return lax.ppermute(value, axes, number)

    def join(mine, sibling):
        first = jnp.where(core == 0, mine, sibling)
        second = jnp.where(core == 0, sibling, mine)
        return jnp.concatenate([first, second], axis=1)

    core_flip = [((r, p, x), (r ^ 1, p, x)) for r, p, x in devices]
    chip_flip = [((r, p, x), (r ^ 2, p, x)) for r, p, x in devices]

    shard = whiten(spectra, 1)[0]
    joined = join(shard, send(shard, core_flip))
    across = send(shard, chip_flip)
    joined_across = join(across, send(across, core_flip))
    offsets = jnp.stack([2 * chip * width, 2 * (1 - chip) * width]).astype(jnp.int32)
    right, out = weights(offsets, [joined, joined_across], sides * rows * width)

    def climb(value, d):
        return send(
            value,
            [
                ((r, p, x), (r, p + 1, x))
                for r, p, x in devices
                if p + 1 < rows and p - d + 1 >= 0 and (p - d + 1 - r) % 2 == 0
            ],
        )

    def to_row(value, depths, flip_side, flip_chip):
        takers = [(r, p, x) for r, p, x in devices if p - r in depths]
        return send(value, [((r ^ 2 * flip_chip, p, x ^ flip_side), (r, p, x)) for r, p, x in takers])

    after = lax.optimization_barrier
    once = climb(joined, 1)
    twice = climb(once, 2)
    side_early = to_row(jnp.where(depth == 0, joined, once), (0, 1), 1, 0)
    chip_one = to_row(once, (1,), 0, 1)
    both_early = to_row(jnp.where(plane == (row_id ^ 2), joined, once), (0, 1), 1, 1)
    twice, side_early, right, table = after((twice, side_early, right, table))
    thrice = climb(twice, 3)
    side_two = to_row(twice, (2,), 1, 0)
    chip_two = to_row(twice, (2,), 0, 1)
    thrice, chip_one, both_early, side_two, chip_two, twice = after(
        (thrice, chip_one, both_early, side_two, chip_two, twice)
    )
    chip_three = to_row(thrice, (3,), 0, 1)
    side_three = to_row(thrice, (3,), 1, 0)
    both_two = to_row(twice, (2,), 1, 1)

    wanted = request == 1
    by_depth = jnp.where(wanted, depth, -1)
    by_late = jnp.where(wanted, jnp.maximum(depth - 1, 0), -1)

    def place(flip_side, flip_chip):
        return ((side ^ flip_side) * rows + 2 * (chip ^ flip_chip)) * width

    out = pair_block(by_depth, place(0, 0), [joined, once, twice, thrice], right, table, out)
    chip_three, out = after((chip_three, out))
    both_three = to_row(chip_three, (3,), 1, 0)
    out = pair_block(by_late, place(1, 0), [side_early, side_two, side_three], right, table, out)
    out = pair_block(by_depth, place(0, 1), [joined_across, chip_one, chip_two, chip_three], right, table, out)
    return pair_block(by_late, place(1, 1), [both_early, both_two, both_three], right, table, out)


def gather_body(spectra, request, table):
    shard = whiten(spectra, 1)[0]
    width = shard.shape[1]
    rows = lax.axis_size("row")
    sides = lax.axis_size("side")
    column = lax.all_gather(shard, "row", axis=1, tiled=True)
    grouped = lax.all_gather(shard, ("plane", "side"), axis=0).reshape(rows, sides, ROWS, width, 128)
    moved = lax.all_to_all(grouped, "row", split_axis=0, concat_axis=0)
    block = jnp.transpose(moved, (2, 1, 0, 3, 4)).reshape(ROWS, sides * rows * width, 128)
    right, out = weights(jnp.zeros((1,), jnp.int32), [column], block.shape[1])
    group = min(64, block.shape[1])
    for at in range(0, block.shape[1], group):
        out = pair_block(request - 1, jnp.int32(at), [block[:, at : at + group]], right, table, out)
    return out


def body(spectra, pair_mask, band_range):
    rows = lax.axis_size("row")
    sides = lax.axis_size("side")
    width = spectra.shape[2]
    request = ((pair_mask[0, 0] == 1) & (lax.axis_index("plane") >= lax.axis_index("row"))).astype(jnp.int32)
    table = make_table(band_range)
    if (rows, sides) == (4, 2) and width % 32 == 0:
        out = relay_body(spectra, request, table)
    else:
        out = gather_body(spectra, request, table)
    return jnp.transpose(out, (1, 2, 0))


def solution(mesh):
    rows, cols = mesh.devices.shape
    cut = Mesh(mesh.devices.reshape(rows, rows, cols // rows), ("row", "plane", "side"))
    return jax.shard_map(
        body,
        mesh=cut,
        in_specs=(P(None, None, ("plane", "side", "row"), None), P("row", ("plane", "side")), P()),
        out_specs=P("row", ("plane", "side"), None),
        check_vma=False,
    )
```

profile of v0, /device:TPU:26, one launch (start us, length us, event | category | flops | bytes accessed | tf_op | source)
XLA Modules:
  0.0 251.1 jit_solution(6829191072297476233)
XLA Ops:
  0.0 1.6 copy-done.1
  1.6 7.0 %whiten.1 = bf16[128,32,128]{2,1,0:T(8,128)(2,1)S(1)} custom-call(f32[1024,512]{1,0:T(8,128)S(1)} %bitcast.13, f32[1024,512]{1,0:T(8,128)S(1)} %bitcast.14, f32[1024,512]{1,0:T(8,128)S(1)} %bitcast.15, f32[1024,512]{1,0:T(8,128)S(1)} %bitcast.16), custom_call_target="tpu_custom_call" | custom-call | tf_op jit(solution)/shard_map/whiten/pallas_call | solution.py:51
  8.6 0.1 collective-permute-start
  8.7 2.6 %collective-permute-done = bf16[128,32,128]{2,1,0:T(8,128)(2,1)S(1)} collective-permute-done((bf16[128,32,128]{2,1,0:T(8,128)(2,1)S(1)}, bf16[128,32,128]{2,1,0:T(8,128)(2,1)S(1)}, u32[]{:S(2)}, u32[]{:S(2)}) %collective-permute-start) | collective-permute-done | bytes 1048608 | tf_op jit(solution)/shard_map/ppermute | solution.py:240
  11.3 0.1 broadcast_select_fusion.5
  11.4 0.0 copy-start.4
  11.4 0.0 copy-start.5
  11.5 0.3 pad_maximum_fusion.refs_0_
  11.7 0.7 copy-done.4
  12.4 0.3 copy-done.5
  12.8 1.3 collective-permute-start.1
  14.0 1.6 collective-permute-start.4
  15.6 25.1 %collective-permute-done.1.refs_1_ = bf16[128,64,128]{2,1,0:T(8,128)(2,1)} collective-permute-done((bf16[128,64,128]{2,1,0:T(8,128)(2,1)S(1)}, bf16[128,64,128]{2,1,0:T(8,128)(2,1)}, u32[]{:S(2)}, u32[]{:S(2)}) %collective-permute-start.1) | collective-permute-done | bytes 2097184 | tf_op jit(solution)/shard_map/ppermute | solution.py:240
  40.8 5.6 %broadcast_select_fusion = (bf16[128,64,128]{2,1,0:T(8,128)(2,1)}, bf16[128,64,128]{2,1,0:T(8,128)(2,1)}) fusion(bf16[128,64,128]{2,1,0:T(8,128)(2,1)} %collective-permute-done.1.refs_1_, pred[]{:T(512)S(6)} %eq.32, bf16[128,32,128]{2,1,0:T(8,128)(2,1)} %copy-done.5, bf16[128,32,128]{2,1,0:T(8,128)(2,1)} %copy-done.4, pred[]{:T(512)S(6)} %eq.31), kind=kLoop, calls=%fused_computation.2 | loop fusion | flops 6291456 | bytes 8388610 | tf_op jit(solution)/shard_map/jit(_where)/select_n | solution.py:276
  46.3 2.0 collective-permute-start.3
  48.4 2.0 collective-permute-start.2
  50.4 0.0 collective-permute-done.4
  50.4 0.0 collective-permute-start.5
  50.4 0.1 pad_add_fusion.1.offset_ref
  50.5 0.0 copy-done.9
  50.5 0.6 fusion.15
  51.1 1.2 fusion.14
  52.3 1.2 and_convert_fusion
  53.5 2.0 multiply_convert_fusion.1
  55.5 0.8 pad_maximum_fusion.2.refs_5_.refs_4_
  56.3 0.0 collective-permute-done.5
  56.3 1.4 broadcast_select_fusion.3
  57.7 0.3 pad_maximum_fusion.1.refs_1_.refs_0_
  58.0 0.0 copy-done.2
  58.0 0.0 copy-start.3
  58.0 0.0 copy-start.7
  58.1 9.0 %weights.1 = (bf16[64,256,256]{2,1,0:T(8,128)(2,1)S(1)}, bf16[201,256,128]{2,1,0:T(8,128)(2,1)}) custom-call(s32[2]{0:T(128)S(1)} %pad_add_fusion.1.offset_ref, bf16[128,64,128]{2,1,0:T(8,128)(2,1)S(1)} %pad_maximum_fusion.refs_0_, bf16[128,64,128]{2,1,0:T(8,128)(2,1)S(1)} %pad_maximum_fusion.1.refs_1_.refs_0_), custom_call_target="tpu_custom_call" | custom-call | tf_op jit(solution)/shard_map/weights/pallas_call | solution.py:89
  67.0 0.0 copy-done.3
  67.0 3.3 %copy-done = bf16[64,256,256]{2,1,0:T(8,128)(2,1)} copy-done((bf16[64,256,256]{2,1,0:T(8,128)(2,1)}, bf16[64,256,256]{2,1,0:T(8,128)(2,1)S(1)}, u32[]{:S(2)}) %copy-start) | copy-done | bytes 8388632
  70.3 4.9 %collective-permute-start.8 = (bf16[128,64,128]{2,1,0:T(8,128)(2,1)S(1)}, bf16[128,64,128]{2,1,0:T(8,128)(2,1)S(1)}, u32[]{:S(2)}, u32[]{:S(2)}) collective-permute-start(bf16[128,64,128]{2,1,0:T(8,128)(2,1)S(1)} %copy-done.7), channel_id=1, source_target_pairs={{17,0},{16,1},{19,2},{18,3},{27,10},{26,11},{29,12},{28,13},{5,20}... | collective-permute-start | bytes 6291464 | tf_op jit(solution)/shard_map/ppermute | solution.py:240
  75.2 2.6 %collective-permute-start.7 = (bf16[128,64,128]{2,1,0:T(8,128)(2,1)}, bf16[128,64,128]{2,1,0:T(8,128)(2,1)}, u32[]{:S(2)}, u32[]{:S(2)}) collective-permute-start(bf16[128,64,128]{2,1,0:T(8,128)(2,1)} %collective-permute-done.1.refs_1_), channel_id=1, source_target_pairs={{18,2},{19,3},{28,12},{29,13},{6,22},{7,23}} | collective-permute-start | bytes 6291464 | tf_op jit(solution)/shard_map/ppermute | solution.py:240
  77.9 0.0 collective-permute-done.3.refs_0_
  77.9 0.0 collective-permute-done.2.refs_2_
  77.9 2.0 collective-permute-start.10
  79.8 2.0 collective-permute-start.9
  81.8 1.3 collective-permute-start.6
  83.1 38.0 %collective-permute-done.8.refs_0_ = bf16[128,64,128]{2,1,0:T(8,128)(2,1)S(1)} collective-permute-done((bf16[128,64,128]{2,1,0:T(8,128)(2,1)S(1)}, bf16[128,64,128]{2,1,0:T(8,128)(2,1)S(1)}, u32[]{:S(2)}, u32[]{:S(2)}) %collective-permute-start.8) | collective-permute-done | bytes 2097184 | tf_op jit(solution)/shard_map/ppermute | solution.py:240
  121.1 22.1 %collective-permute-done.7.refs_1_ = bf16[128,64,128]{2,1,0:T(8,128)(2,1)} collective-permute-done((bf16[128,64,128]{2,1,0:T(8,128)(2,1)}, bf16[128,64,128]{2,1,0:T(8,128)(2,1)}, u32[]{:S(2)}, u32[]{:S(2)}) %collective-permute-start.7) | collective-permute-done | bytes 2097184 | tf_op jit(solution)/shard_map/ppermute | solution.py:240
  143.2 0.0 collective-permute-done.10.refs_2_
  143.2 0.0 collective-permute-done.9.refs_1_
  143.2 0.0 collective-permute-done.6.refs_3_
  143.2 1.3 collective-permute-start.12
  144.5 3.4 %collective-permute-start.14 = (bf16[128,64,128]{2,1,0:T(8,128)(2,1)}, bf16[128,64,128]{2,1,0:T(8,128)(2,1)}, u32[]{:S(2)}, u32[]{:S(2)}) collective-permute-start(bf16[128,64,128]{2,1,0:T(8,128)(2,1)} %collective-permute-done.6.refs_3_), channel_id=1, source_target_pairs={{7,6},{6,7}} | collective-permute-start | bytes 6291464 | tf_op jit(solution)/shard_map/ppermute | solution.py:240
  148.6 0.6 pad_add_fusion.2.meta_ref
  149.1 2.0 collective-permute-start.11
  151.2 16.7 %pair_block.4.refs_5_ = bf16[201,256,128]{2,1,0:T(8,128)(2,1)} custom-call(s32[2]{0:T(128)} %pad_add_fusion.2.meta_ref, bf16[128,64,128]{2,1,0:T(8,128)(2,1)} %copy-done.2, bf16[128,64,128]{2,1,0:T(8,128)(2,1)} %collective-permute-done.1.refs_1_, bf16[128,64,128]{2,1,0:T(8,128)(2,1)} %collective-permute-done.2.refs_2_, ...), custom_call_target="tpu_custom_call", output_to_operand_aliasing={{}: (7, {})} | custom-call | flops 7784628224 | bytes 11681792 | tf_op jit(solution)/shard_map/pair_block/pallas_call | solution.py:182
  167.9 0.0 copy-done.6
  167.9 26.0 %collective-permute-done.12.refs_3_ = bf16[128,64,128]{2,1,0:T(8,128)(2,1)} collective-permute-done((bf16[128,64,128]{2,1,0:T(8,128)(2,1)}, bf16[128,64,128]{2,1,0:T(8,128)(2,1)}, u32[]{:S(2)}, u32[]{:S(2)}) %collective-permute-start.12) | collective-permute-done | bytes 2097184 | tf_op jit(solution)/shard_map/ppermute | solution.py:240
  193.9 3.4 %collective-permute-start.13 = (bf16[128,64,128]{2,1,0:T(8,128)(2,1)}, bf16[128,64,128]{2,1,0:T(8,128)(2,1)S(1)}, u32[]{:S(2)}, u32[]{:S(2)}) collective-permute-start(bf16[128,64,128]{2,1,0:T(8,128)(2,1)} %collective-permute-done.12.refs_3_), channel_id=1, source_target_pairs={{7,6},{6,7}} | collective-permute-start | bytes 6291464 | tf_op jit(solution)/shard_map/ppermute | solution.py:240
  197.3 0.6 pad_add_fusion.4.meta_ref
  197.9 0.6 pad_add_fusion.meta_ref
  198.5 0.7 pad_add_fusion.3.meta_ref
  199.2 0.0 collective-permute-done.14.refs_2_
  199.2 16.7 %pair_block.5.refs_6_ = bf16[201,256,128]{2,1,0:T(8,128)(2,1)} custom-call(s32[2]{0:T(128)} %pad_add_fusion.4.meta_ref, bf16[128,64,128]{2,1,0:T(8,128)(2,1)} %collective-permute-done.3.refs_0_, bf16[128,64,128]{2,1,0:T(8,128)(2,1)} %collective-permute-done.9.refs_1_, ...), custom_call_target="tpu_custom_call", output_to_operand_aliasing={{}: (6, {})} | custom-call | flops 7784628224 | bytes 11681792 | tf_op jit(solution)/shard_map/pair_block/pallas_call | solution.py:182
  215.9 16.9 %pair_block.6.refs_5_ = bf16[201,256,128]{2,1,0:T(8,128)(2,1)} custom-call(s32[2]{0:T(128)} %pad_add_fusion.3.meta_ref, bf16[128,64,128]{2,1,0:T(8,128)(2,1)} %copy-done.3, bf16[128,64,128]{2,1,0:T(8,128)(2,1)} %collective-permute-done.7.refs_1_, bf16[128,64,128]{2,1,0:T(8,128)(2,1)} %collective-permute-done.10.refs_2_, ...), custom_call_target="tpu_custom_call", output_to_operand_aliasing={{}: (7, {})} | custom-call | flops 7784628224 | bytes 11681792 | tf_op jit(solution)/shard_map/pair_block/pallas_call | solution.py:182
  232.8 0.0 collective-permute-done.11.refs_1_
  232.8 0.0 collective-permute-done.13.refs_2_
  232.9 1.4 copy-done.8
  234.2 16.7 %pair_block.7 = bf16[201,256,128]{2,1,0:T(8,128)(2,1)} custom-call(s32[2]{0:T(128)} %pad_add_fusion.meta_ref, bf16[128,64,128]{2,1,0:T(8,128)(2,1)} %copy-done.6, bf16[128,64,128]{2,1,0:T(8,128)(2,1)} %collective-permute-done.11.refs_1_, bf16[128,64,128]{2,1,0:T(8,128)(2,1)} %copy-done.8, ...), custom_call_target="tpu_custom_call", output_to_operand_aliasing={{}: (6, {})} | custom-call | flops 7784628224 | bytes 11681792 | tf_op jit(solution)/shard_map/pair_block/pallas_call | solution.py:182
  (9 shorter events, 0.0 us)
Async XLA Ops:
  0.0 1.6 copy-start.1
  8.6 2.7 %collective-permute-start = (bf16[128,32,128]{2,1,0:T(8,128)(2,1)S(1)}, bf16[128,32,128]{2,1,0:T(8,128)(2,1)S(1)}, u32[]{:S(2)}, u32[]{:S(2)}) collective-permute-start(bf16[128,32,128]{2,1,0:T(8,128)(2,1)S(1)} %whiten.1), channel_id=1, source_target_pairs={{0,8},{1,9},{2,10},{3,11},{4,12},{5,13},{6,14},{7,15},{8,0},{9,1},... | collective-permute-start | bytes 3145736 | tf_op jit(solution)/shard_map/ppermute | solution.py:240
  11.4 1.0 copy-start.4
  11.4 1.3 copy-start.5
  12.7 45.3 %copy-start.2 = (bf16[128,64,128]{2,1,0:T(8,128)(2,1)}, bf16[128,64,128]{2,1,0:T(8,128)(2,1)S(1)}, u32[]{:S(2)}) copy-start(bf16[128,64,128]{2,1,0:T(8,128)(2,1)S(1)} %pad_maximum_fusion.refs_0_) | copy-start | bytes 6291460
  12.8 28.0 %collective-permute-start.1 = (bf16[128,64,128]{2,1,0:T(8,128)(2,1)S(1)}, bf16[128,64,128]{2,1,0:T(8,128)(2,1)}, u32[]{:S(2)}, u32[]{:S(2)}) collective-permute-start(bf16[128,64,128]{2,1,0:T(8,128)(2,1)S(1)} %pad_maximum_fusion.refs_0_), channel_id=1, source_target_pairs={{0,2},{1,3},{4,6},{5,7},{10,12},{11,13},{16,18},{17,19},{20,22},{2... | collective-permute-start | bytes 6291464 | tf_op jit(solution)/shard_map/ppermute | solution.py:240
  14.0 36.4 %collective-permute-start.4 = (bf16[128,32,128]{2,1,0:T(8,128)(2,1)S(1)}, bf16[128,32,128]{2,1,0:T(8,128)(2,1)}, u32[]{:S(2)}, u32[]{:S(2)}) collective-permute-start(bf16[128,32,128]{2,1,0:T(8,128)(2,1)S(1)} %whiten.1), channel_id=1, source_target_pairs={{0,16},{1,17},{2,18},{3,19},{4,20},{5,21},{6,22},{7,23},{8,24},{9,... | collective-permute-start | bytes 3145736 | tf_op jit(solution)/shard_map/ppermute | solution.py:240
  15.6 34.9 %copy-start.9 = (s32[2]{0:T(128)S(1)}, s32[2]{0:T(128)}, u32[]{:S(2)}) copy-start(s32[2]{0:T(128)} %param.5) | copy-start | bytes 28
  46.3 31.5 %collective-permute-start.3 = (bf16[128,64,128]{2,1,0:T(8,128)(2,1)}, bf16[128,64,128]{2,1,0:T(8,128)(2,1)}, u32[]{:S(2)}, u32[]{:S(2)}) collective-permute-start(bf16[128,64,128]{2,1,0:T(8,128)(2,1)} %get-tuple-element.34), channel_id=1, source_target_pairs={{1,0},{0,1},{3,2},{2,3},{11,10},{10,11},{13,12},{12,13},{21,20},{2... | collective-permute-start | bytes 6291464 | tf_op jit(solution)/shard_map/ppermute | solution.py:240
  48.4 29.5 %collective-permute-start.2 = (bf16[128,64,128]{2,1,0:T(8,128)(2,1)}, bf16[128,64,128]{2,1,0:T(8,128)(2,1)}, u32[]{:S(2)}, u32[]{:S(2)}) collective-permute-start(bf16[128,64,128]{2,1,0:T(8,128)(2,1)} %collective-permute-done.1.refs_1_), channel_id=1, source_target_pairs={{2,4},{3,5},{12,14},{13,15},{18,20},{19,21},{28,30},{29,31}} | collective-permute-start | bytes 6291464 | tf_op jit(solution)/shard_map/ppermute | solution.py:240
  50.4 6.0 %collective-permute-start.5 = (bf16[128,32,128]{2,1,0:T(8,128)(2,1)}, bf16[128,32,128]{2,1,0:T(8,128)(2,1)S(1)}, u32[]{:S(2)}, u32[]{:S(2)}) collective-permute-start(bf16[128,32,128]{2,1,0:T(8,128)(2,1)} %collective-permute-done.4), channel_id=1, source_target_pairs={{0,8},{1,9},{2,10},{3,11},{4,12},{5,13},{6,14},{7,15},{8,0},{9,1},... | collective-permute-start | bytes 3145736 | tf_op jit(solution)/shard_map/ppermute | solution.py:240
  58.0 9.0 %copy-start.3 = (bf16[128,64,128]{2,1,0:T(8,128)(2,1)}, bf16[128,64,128]{2,1,0:T(8,128)(2,1)S(1)}, u32[]{:S(2)}) copy-start(bf16[128,64,128]{2,1,0:T(8,128)(2,1)S(1)} %pad_maximum_fusion.1.refs_1_.refs_0_) | copy-start | bytes 6291460
  58.0 12.2 %copy-start.7 = (bf16[128,64,128]{2,1,0:T(8,128)(2,1)S(1)}, bf16[128,64,128]{2,1,0:T(8,128)(2,1)}, u32[]{:S(2)}) copy-start(bf16[128,64,128]{2,1,0:T(8,128)(2,1)} %get-tuple-element.33) | copy-start | bytes 6291460
  67.0 3.3 %copy-start = (bf16[64,256,256]{2,1,0:T(8,128)(2,1)}, bf16[64,256,256]{2,1,0:T(8,128)(2,1)S(1)}, u32[]{:S(2)}) copy-start(bf16[64,256,256]{2,1,0:T(8,128)(2,1)S(1)} %get-tuple-element.24.refs_4_.refs_3_) | copy-start | bytes 25165828
  70.3 50.8 %collective-permute-start.8 = (bf16[128,64,128]{2,1,0:T(8,128)(2,1)S(1)}, bf16[128,64,128]{2,1,0:T(8,128)(2,1)S(1)}, u32[]{:S(2)}, u32[]{:S(2)}) collective-permute-start(bf16[128,64,128]{2,1,0:T(8,128)(2,1)S(1)} %copy-done.7), channel_id=1, source_target_pairs={{17,0},{16,1},{19,2},{18,3},{27,10},{26,11},{29,12},{28,13},{5,20}... | collective-permute-start | bytes 6291464 | tf_op jit(solution)/shard_map/ppermute | solution.py:240
  75.2 68.0 %collective-permute-start.7 = (bf16[128,64,128]{2,1,0:T(8,128)(2,1)}, bf16[128,64,128]{2,1,0:T(8,128)(2,1)}, u32[]{:S(2)}, u32[]{:S(2)}) collective-permute-start(bf16[128,64,128]{2,1,0:T(8,128)(2,1)} %collective-permute-done.1.refs_1_), channel_id=1, source_target_pairs={{18,2},{19,3},{28,12},{29,13},{6,22},{7,23}} | collective-permute-start | bytes 6291464 | tf_op jit(solution)/shard_map/ppermute | solution.py:240
  77.9 65.3 %collective-permute-start.10 = (bf16[128,64,128]{2,1,0:T(8,128)(2,1)}, bf16[128,64,128]{2,1,0:T(8,128)(2,1)}, u32[]{:S(2)}, u32[]{:S(2)}) collective-permute-start(bf16[128,64,128]{2,1,0:T(8,128)(2,1)} %collective-permute-done.2.refs_2_), channel_id=1, source_target_pairs={{20,4},{21,5},{30,14},{31,15}} | collective-permute-start | bytes 6291464 | tf_op jit(solution)/shard_map/ppermute | solution.py:240
  79.8 63.3 %collective-permute-start.9 = (bf16[128,64,128]{2,1,0:T(8,128)(2,1)}, bf16[128,64,128]{2,1,0:T(8,128)(2,1)}, u32[]{:S(2)}, u32[]{:S(2)}) collective-permute-start(bf16[128,64,128]{2,1,0:T(8,128)(2,1)} %collective-permute-done.2.refs_2_), channel_id=1, source_target_pairs={{5,4},{4,5},{15,14},{14,15}} | collective-permute-start | bytes 6291464 | tf_op jit(solution)/shard_map/ppermute | solution.py:240
  81.8 61.4 %collective-permute-start.6 = (bf16[128,64,128]{2,1,0:T(8,128)(2,1)}, bf16[128,64,128]{2,1,0:T(8,128)(2,1)}, u32[]{:S(2)}, u32[]{:S(2)}) collective-permute-start(bf16[128,64,128]{2,1,0:T(8,128)(2,1)} %collective-permute-done.2.refs_2_), channel_id=1, source_target_pairs={{4,6},{5,7},{20,22},{21,23}} | collective-permute-start | bytes 6291464 | tf_op jit(solution)/shard_map/ppermute | solution.py:240
  121.1 46.8 %copy-start.6 = (bf16[128,64,128]{2,1,0:T(8,128)(2,1)}, bf16[128,64,128]{2,1,0:T(8,128)(2,1)S(1)}, u32[]{:S(2)}) copy-start(bf16[128,64,128]{2,1,0:T(8,128)(2,1)S(1)} %collective-permute-done.8.refs_0_) | copy-start | bytes 6291460
  143.2 50.7 %collective-permute-start.12 = (bf16[128,64,128]{2,1,0:T(8,128)(2,1)}, bf16[128,64,128]{2,1,0:T(8,128)(2,1)}, u32[]{:S(2)}, u32[]{:S(2)}) collective-permute-start(bf16[128,64,128]{2,1,0:T(8,128)(2,1)} %collective-permute-done.6.refs_3_), channel_id=1, source_target_pairs={{22,6},{23,7}} | collective-permute-start | bytes 6291464 | tf_op jit(solution)/shard_map/ppermute | solution.py:240
  144.5 54.7 %collective-permute-start.14 = (bf16[128,64,128]{2,1,0:T(8,128)(2,1)}, bf16[128,64,128]{2,1,0:T(8,128)(2,1)}, u32[]{:S(2)}, u32[]{:S(2)}) collective-permute-start(bf16[128,64,128]{2,1,0:T(8,128)(2,1)} %collective-permute-done.6.refs_3_), channel_id=1, source_target_pairs={{7,6},{6,7}} | collective-permute-start | bytes 6291464 | tf_op jit(solution)/shard_map/ppermute | solution.py:240
  149.1 83.7 %collective-permute-start.11 = (bf16[128,64,128]{2,1,0:T(8,128)(2,1)}, bf16[128,64,128]{2,1,0:T(8,128)(2,1)}, u32[]{:S(2)}, u32[]{:S(2)}) collective-permute-start(bf16[128,64,128]{2,1,0:T(8,128)(2,1)} %collective-permute-done.2.refs_2_), channel_id=1, source_target_pairs={{21,4},{20,5},{31,14},{30,15}} | collective-permute-start | bytes 6291464 | tf_op jit(solution)/shard_map/ppermute | solution.py:240
  193.9 39.0 %collective-permute-start.13 = (bf16[128,64,128]{2,1,0:T(8,128)(2,1)}, bf16[128,64,128]{2,1,0:T(8,128)(2,1)S(1)}, u32[]{:S(2)}, u32[]{:S(2)}) collective-permute-start(bf16[128,64,128]{2,1,0:T(8,128)(2,1)} %collective-permute-done.12.refs_3_), channel_id=1, source_target_pairs={{7,6},{6,7}} | collective-permute-start | bytes 6291464 | tf_op jit(solution)/shard_map/ppermute | solution.py:240
  232.9 1.4 copy-start.8
where the time goes:
time: 252 us; the launch traced here: 251 us
  waiting for transfers between devices  114 us (45%)
  Pallas kernels  83 us (33%)
  starting transfers between devices  29.9 us (12%)
  other arithmetic  15.4 us (6%)
  local copies, waits for them, and re-layouts  7.88 us (3%)
    ppermute x15, waiting for transfers between devices, send(): return lax.ppermute(value, axes, number)  114 us
    pallas_call x4, Pallas kernels, pair_block(): pl.pallas_call(functools.partial(pair_kernel, count=count, height=height,...  67 us
    ppermute x15, starting transfers between devices, send(): return lax.ppermute(value, axes, number)  29.9 us
    pallas_call x1, Pallas kernels, weights(): pl.pallas_call(functools.partial(weights_kernel, count=count, step=step),...  8.96 us
    unnamed x20, local copies, waits for them, and re-layouts  7.29 us
    pallas_call x1, Pallas kernels, whiten(): pl.pallas_call(functools.partial(whiten_kernel, width=width, parts=parts)...  6.96 us
    select_n x1, other arithmetic, relay_body(): jnp.where(plane == row_id ^ 2, joined, once)  5.56 us
  transfers between devices with their start and end apart: 15, of which 5 were waited for; matrix products, arithmetic and copies ran while one was open for 6% of the time, Pallas kernels for 24%

commit v1 on v0

--- a/solution.py
+++ b/solution.py
@@ -264,40 +264,38 @@
             ],
         )
 
-    def to_row(value, depths, flip_side, flip_chip):
-        takers = [(r, p, x) for r, p, x in devices if p - r in depths]
+    def to_row(value, d, flip_side, flip_chip):
+        takers = [(r, p, x) for r, p, x in devices if p - r == d]
         return send(value, [((r ^ 2 * flip_chip, p, x ^ flip_side), (r, p, x)) for r, p, x in takers])
 
     after = lax.optimization_barrier
     once = climb(joined, 1)
+    side_zero = to_row(joined, 0, 1, 0)
+    both_zero = to_row(joined_across, 0, 1, 0)
     twice = climb(once, 2)
-    side_early = to_row(jnp.where(depth == 0, joined, once), (0, 1), 1, 0)
-    chip_one = to_row(once, (1,), 0, 1)
-    both_early = to_row(jnp.where(plane == (row_id ^ 2), joined, once), (0, 1), 1, 1)
-    twice, side_early, right, table = after((twice, side_early, right, table))
+    chip_one = to_row(once, 1, 0, 1)
+    side_one = to_row(once, 1, 1, 0)
+    twice, side_zero, both_zero, chip_one, right, table = after((twice, side_zero, both_zero, chip_one, right, table))
     thrice = climb(twice, 3)
-    side_two = to_row(twice, (2,), 1, 0)
-    chip_two = to_row(twice, (2,), 0, 1)
-    thrice, chip_one, both_early, side_two, chip_two, twice = after(
-        (thrice, chip_one, both_early, side_two, chip_two, twice)
-    )
-    chip_three = to_row(thrice, (3,), 0, 1)
-    side_three = to_row(thrice, (3,), 1, 0)
-    both_two = to_row(twice, (2,), 1, 1)
-
-    wanted = request == 1
-    by_depth = jnp.where(wanted, depth, -1)
-    by_late = jnp.where(wanted, jnp.maximum(depth - 1, 0), -1)
+    chip_two = to_row(twice, 2, 0, 1)
+    side_two = to_row(twice, 2, 1, 0)
+    both_one = to_row(chip_one, 1, 1, 0)
+    thrice, side_one, side_two, chip_two, twice = after((thrice, side_one, side_two, chip_two, twice))
+    chip_three = to_row(thrice, 3, 0, 1)
+    side_three = to_row(thrice, 3, 1, 0)
+    both_two = to_row(twice, 2, 1, 1)
+
+    by_depth = jnp.where(request == 1, depth, -1)
 
     def place(flip_side, flip_chip):
         return ((side ^ flip_side) * rows + 2 * (chip ^ flip_chip)) * width
 
     out = pair_block(by_depth, place(0, 0), [joined, once, twice, thrice], right, table, out)
     chip_three, out = after((chip_three, out))
-    both_three = to_row(chip_three, (3,), 1, 0)
-    out = pair_block(by_late, place(1, 0), [side_early, side_two, side_three], right, table, out)
+    both_three = to_row(chip_three, 3, 1, 0)
+    out = pair_block(by_depth, place(1, 0), [side_zero, side_one, side_two, side_three], right, table, out)
     out = pair_block(by_depth, place(0, 1), [joined_across, chip_one, chip_two, chip_three], right, table, out)
-    return pair_block(by_late, place(1, 1), [both_early, both_two, both_three], right, table, out)
+    return pair_block(by_depth, place(1, 1), [both_zero, both_one, both_two, both_three], right, table, out)
 
 
 def gather_body(spectra, request, table):

time: 252 us -> 228 us (0.905)
  waiting for transfers between devices: 114 us -> 95.2 us
  other arithmetic: 15.4 us -> 10.3 us
    ppermute x15 -> x17, waiting for transfers between devices: 114 us -> 95.2 us  [send(): return lax.ppermute(value, axes, number)]
    select_n x1 -> x0, other arithmetic: 5.56 us -> none  [relay_body(): jnp.where(plane == row_id ^ 2, joined, once)]
    ppermute x15 -> x17, starting transfers between devices: 29.9 us -> 28.8 us  [send(): return lax.ppermute(value, axes, number)]
    unnamed x20 -> x14, local copies, waits for them, and re-layouts: 7.29 us -> 7.51 us
  transfers between devices with their start and end apart: 15 -> 17, of which waited for: 5 -> 7; matrix products, arithmetic and copies ran while one was open for 6% -> 5% of each run, Pallas kernels for 24% -> 26%
where the time goes in v1:
time: 228 us
  waiting for transfers between devices  95.2 us (42%)
  Pallas kernels  84 us (37%)
  starting transfers between devices  28.8 us (13%)
  other arithmetic  10.3 us (5%)
  local copies, waits for them, and re-layouts  8.17 us (4%)
    ppermute x17, waiting for transfers between devices, send(): return lax.ppermute(value, axes, number)  95.2 us
    pallas_call x4, Pallas kernels, pair_block(): pl.pallas_call(functools.partial(pair_kernel, count=count, height=height,...  67 us
    ppermute x17, starting transfers between devices, send(): return lax.ppermute(value, axes, number)  28.8 us
    pallas_call x1, Pallas kernels, weights(): pl.pallas_call(functools.partial(weights_kernel, count=count, step=step),...  9.98 us
    unnamed x14, local copies, waits for them, and re-layouts  7.51 us
    pallas_call x1, Pallas kernels, whiten(): pl.pallas_call(functools.partial(whiten_kernel, width=width, parts=parts)...  6.96 us
  transfers between devices with their start and end apart: 17, of which 7 were waited for; matrix products, arithmetic and copies ran while one was open for 5% of the time, Pallas kernels for 26%

profile of v1, /device:TPU:26, one launch (start us, length us, event | category | flops | bytes accessed | tf_op | source)
XLA Modules:
  0.0 227.6 jit_solution(17724561108028185860)
XLA Ops:
  0.0 1.6 copy-done.1
  1.6 7.0 %whiten.1 = bf16[128,32,128]{2,1,0:T(8,128)(2,1)S(1)} custom-call(f32[1024,512]{1,0:T(8,128)S(1)} %bitcast.12, f32[1024,512]{1,0:T(8,128)S(1)} %bitcast.13, f32[1024,512]{1,0:T(8,128)S(1)} %bitcast.14, f32[1024,512]{1,0:T(8,128)S(1)} %bitcast.15), custom_call_target="tpu_custom_call" | custom-call | tf_op jit(solution)/shard_map/whiten/pallas_call | solution.py:51
  8.6 0.1 collective-permute-start
  8.6 1.6 collective-permute-start.4
  10.2 1.1 collective-permute-done
  11.3 0.1 broadcast_select_fusion.3
  11.4 1.6 pad_maximum_fusion.refs_0_
  13.0 1.3 collective-permute-start.1
  14.3 19.9 %collective-permute-done.4 = bf16[128,32,128]{2,1,0:T(8,128)(2,1)S(1)} collective-permute-done((bf16[128,32,128]{2,1,0:T(8,128)(2,1)S(1)}, bf16[128,32,128]{2,1,0:T(8,128)(2,1)S(1)}, u32[]{:S(2)}, u32[]{:S(2)}) %collective-permute-start.4) | collective-permute-done | bytes 1048608 | tf_op jit(solution)/shard_map/ppermute | solution.py:240
  34.2 0.0 collective-permute-start.5
  34.2 2.0 collective-permute-start.3
  36.2 0.7 collective-permute-done.5
  36.9 0.1 broadcast_select_fusion.1
  37.0 0.0 copy-start.6
  37.0 0.3 pad_maximum_fusion.1.refs_1_.refs_0_
  37.3 0.0 copy-start.2
  37.3 2.1 collective-permute-start.6
  39.4 1.9 collective-permute-done.1.refs_1_
  41.3 2.0 collective-permute-start.2
  43.3 4.7 %collective-permute-start.7 = (bf16[128,64,128]{2,1,0:T(8,128)(2,1)}, bf16[128,64,128]{2,1,0:T(8,128)(2,1)}, u32[]{:S(2)}, u32[]{:S(2)}) collective-permute-start(bf16[128,64,128]{2,1,0:T(8,128)(2,1)} %collective-permute-done.1.refs_1_), channel_id=1, source_target_pairs={{18,2},{19,3},{28,12},{29,13},{6,22},{7,23}} | collective-permute-start | bytes 6291464 | tf_op jit(solution)/shard_map/ppermute | solution.py:240
  48.0 0.1 pad_add_fusion.1.offset_ref
  48.1 0.0 copy-done.6
  48.1 0.7 fusion.15
  48.7 1.3 and_convert_fusion
  50.1 1.3 fusion.14
  51.4 2.0 multiply_convert_fusion.1
  53.4 0.8 pad_maximum_fusion.2.refs_5_
  54.2 10.0 %weights.1 = (bf16[64,256,256]{2,1,0:T(8,128)(2,1)S(1)}, bf16[201,256,128]{2,1,0:T(8,128)(2,1)}) custom-call(s32[2]{0:T(128)S(1)} %pad_add_fusion.1.offset_ref, bf16[128,64,128]{2,1,0:T(8,128)(2,1)} %pad_maximum_fusion.refs_0_, bf16[128,64,128]{2,1,0:T(8,128)(2,1)S(1)} %pad_maximum_fusion.1.refs_1_.refs_0_), custom_call_target="tpu_custom_call" | custom-call | tf_op jit(solution)/shard_map/weights/pallas_call | solution.py:89
  64.2 0.0 copy-done.2
  64.2 3.3 %copy-done = bf16[64,256,256]{2,1,0:T(8,128)(2,1)} copy-done((bf16[64,256,256]{2,1,0:T(8,128)(2,1)}, bf16[64,256,256]{2,1,0:T(8,128)(2,1)S(1)}, u32[]{:S(2)}) %copy-start) | copy-done | bytes 8388632
  67.5 2.0 collective-permute-start.10
  69.5 0.0 collective-permute-done.3.refs_0_
  69.5 0.0 collective-permute-done.6.refs_0_
  69.5 0.0 collective-permute-done.2.refs_2_
  69.5 1.0 collective-permute-done.7.refs_1_
  70.5 0.8 collective-permute-start.11
  71.3 0.8 collective-permute-start.12
  72.1 1.3 collective-permute-start.9
  73.4 0.0 collective-permute-done.10.refs_1_
  73.4 0.0 collective-permute-done.11.refs_2_
  73.5 0.0 copy-start.4
  73.5 0.0 collective-permute-done.12.refs_2_
  73.5 1.3 copy-done.4
  74.8 25.6 %collective-permute-done.9.refs_3_ = bf16[128,64,128]{2,1,0:T(8,128)(2,1)} collective-permute-done((bf16[128,64,128]{2,1,0:T(8,128)(2,1)}, bf16[128,64,128]{2,1,0:T(8,128)(2,1)}, u32[]{:S(2)}, u32[]{:S(2)}) %collective-permute-start.9) | collective-permute-done | bytes 2097184 | tf_op jit(solution)/shard_map/ppermute | solution.py:240
  100.4 1.3 collective-permute-start.14
  101.7 2.4 %collective-permute-start.16 = (bf16[128,64,128]{2,1,0:T(8,128)(2,1)}, bf16[128,64,128]{2,1,0:T(8,128)(2,1)}, u32[]{:S(2)}, u32[]{:S(2)}) collective-permute-start(bf16[128,64,128]{2,1,0:T(8,128)(2,1)} %collective-permute-done.9.refs_3_), channel_id=1, source_target_pairs={{7,6},{6,7}} | collective-permute-start | bytes 6291464 | tf_op jit(solution)/shard_map/ppermute | solution.py:240
  104.8 0.6 pad_add_fusion.2.meta_ref
  105.4 2.0 collective-permute-start.8
  107.4 2.1 collective-permute-start.13
  109.5 16.7 %pair_block.4.refs_6_ = bf16[201,256,128]{2,1,0:T(8,128)(2,1)} custom-call(s32[2]{0:T(128)} %pad_add_fusion.2.meta_ref, bf16[128,64,128]{2,1,0:T(8,128)(2,1)} %pad_maximum_fusion.refs_0_, bf16[128,64,128]{2,1,0:T(8,128)(2,1)} %collective-permute-done.1.refs_1_, bf16[128,64,128]{2,1,0:T(8,128)(2,1)} %collective-permute-done.2.refs_2_, ...), custom_call_target="tpu_custom_call", output_to_operand_aliasing={{}: (7, {})} | custom-call | flops 7784628224 | bytes 11681792 | tf_op jit(solution)/shard_map/pair_block/pallas_call | solution.py:182
  126.2 0.0 copy-done.3
  126.2 45.1 %collective-permute-done.14.refs_3_ = bf16[128,64,128]{2,1,0:T(8,128)(2,1)} collective-permute-done((bf16[128,64,128]{2,1,0:T(8,128)(2,1)}, bf16[128,64,128]{2,1,0:T(8,128)(2,1)}, u32[]{:S(2)}, u32[]{:S(2)}) %collective-permute-start.14) | collective-permute-done | bytes 2097184 | tf_op jit(solution)/shard_map/ppermute | solution.py:240
  171.3 2.4 %collective-permute-start.15 = (bf16[128,64,128]{2,1,0:T(8,128)(2,1)}, bf16[128,64,128]{2,1,0:T(8,128)(2,1)S(1)}, u32[]{:S(2)}, u32[]{:S(2)}) collective-permute-start(bf16[128,64,128]{2,1,0:T(8,128)(2,1)} %collective-permute-done.14.refs_3_), channel_id=1, source_target_pairs={{7,6},{6,7}} | collective-permute-start | bytes 6291464 | tf_op jit(solution)/shard_map/ppermute | solution.py:240
  173.8 0.7 pad_add_fusion.4.meta_ref
  174.4 0.6 pad_add_fusion.3.meta_ref
  175.0 0.7 pad_add_fusion.meta_ref
  175.7 0.0 collective-permute-done.16.refs_3_
  175.7 16.7 %pair_block.5.refs_6_ = bf16[201,256,128]{2,1,0:T(8,128)(2,1)} custom-call(s32[2]{0:T(128)} %pad_add_fusion.4.meta_ref, bf16[128,64,128]{2,1,0:T(8,128)(2,1)} %collective-permute-done.3.refs_0_, bf16[128,64,128]{2,1,0:T(8,128)(2,1)} %collective-permute-done.10.refs_1_, bf16[128,64,128]{2,1,0:T(8,128)(2,1)} %copy-done.4, ...), custom_call_target="tpu_custom_call", output_to_operand_aliasing={{}: (7, {})} | custom-call | flops 7784628224 | bytes 11681792 | tf_op jit(solution)/shard_map/pair_block/pallas_call | solution.py:182
  192.4 16.9 %pair_block.6.refs_6_ = bf16[201,256,128]{2,1,0:T(8,128)(2,1)} custom-call(s32[2]{0:T(128)} %pad_add_fusion.3.meta_ref, bf16[128,64,128]{2,1,0:T(8,128)(2,1)} %copy-done.2, bf16[128,64,128]{2,1,0:T(8,128)(2,1)} %collective-permute-done.7.refs_1_, bf16[128,64,128]{2,1,0:T(8,128)(2,1)} %copy-done.3, ...), custom_call_target="tpu_custom_call", output_to_operand_aliasing={{}: (7, {})} | custom-call | flops 7784628224 | bytes 11681792 | tf_op jit(solution)/shard_map/pair_block/pallas_call | solution.py:182
  209.3 0.0 collective-permute-done.8.refs_1_
  209.3 0.0 collective-permute-done.13.refs_2_
  209.4 0.0 collective-permute-done.15.refs_3_
  209.4 1.3 copy-done.5
  210.7 16.7 %pair_block.7 = bf16[201,256,128]{2,1,0:T(8,128)(2,1)} custom-call(s32[2]{0:T(128)} %pad_add_fusion.meta_ref, bf16[128,64,128]{2,1,0:T(8,128)(2,1)} %collective-permute-done.6.refs_0_, bf16[128,64,128]{2,1,0:T(8,128)(2,1)} %collective-permute-done.8.refs_1_, bf16[128,64,128]{2,1,0:T(8,128)(2,1)} %collective-permute-done.13.refs_2_, ...), custom_call_target="tpu_custom_call", output_to_operand_aliasing={{}: (7, {})} | custom-call | flops 7784628224 | bytes 11681792 | tf_op jit(solution)/shard_map/pair_block/pallas_call | solution.py:182
  (6 shorter events, 0.0 us)
Async XLA Ops:
  0.0 1.6 copy-start.1
  8.6 2.7 %collective-permute-start = (bf16[128,32,128]{2,1,0:T(8,128)(2,1)S(1)}, bf16[128,32,128]{2,1,0:T(8,128)(2,1)S(1)}, u32[]{:S(2)}, u32[]{:S(2)}) collective-permute-start(bf16[128,32,128]{2,1,0:T(8,128)(2,1)S(1)} %whiten.1), channel_id=1, source_target_pairs={{0,8},{1,9},{2,10},{3,11},{4,12},{5,13},{6,14},{7,15},{8,0},{9,1},... | collective-permute-start | bytes 3145736 | tf_op jit(solution)/shard_map/ppermute | solution.py:240
  8.6 25.6 %collective-permute-start.4 = (bf16[128,32,128]{2,1,0:T(8,128)(2,1)S(1)}, bf16[128,32,128]{2,1,0:T(8,128)(2,1)S(1)}, u32[]{:S(2)}, u32[]{:S(2)}) collective-permute-start(bf16[128,32,128]{2,1,0:T(8,128)(2,1)S(1)} %whiten.1), channel_id=1, source_target_pairs={{0,16},{1,17},{2,18},{3,19},{4,20},{5,21},{6,22},{7,23},{8,24},{9,... | collective-permute-start | bytes 3145736 | tf_op jit(solution)/shard_map/ppermute | solution.py:240
  13.0 28.2 %collective-permute-start.1 = (bf16[128,64,128]{2,1,0:T(8,128)(2,1)}, bf16[128,64,128]{2,1,0:T(8,128)(2,1)}, u32[]{:S(2)}, u32[]{:S(2)}) collective-permute-start(bf16[128,64,128]{2,1,0:T(8,128)(2,1)} %pad_maximum_fusion.refs_0_), channel_id=1, source_target_pairs={{0,2},{1,3},{4,6},{5,7},{10,12},{11,13},{16,18},{17,19},{20,22},{2... | collective-permute-start | bytes 6291464 | tf_op jit(solution)/shard_map/ppermute | solution.py:240
  34.2 2.7 %collective-permute-start.5 = (bf16[128,32,128]{2,1,0:T(8,128)(2,1)S(1)}, bf16[128,32,128]{2,1,0:T(8,128)(2,1)S(1)}, u32[]{:S(2)}, u32[]{:S(2)}) collective-permute-start(bf16[128,32,128]{2,1,0:T(8,128)(2,1)S(1)} %collective-permute-done.4), channel_id=1, source_target_pairs={{0,8},{1,9},{2,10},{3,11},{4,12},{5,13},{6,14},{7,15},{8,0},{9,1},... | collective-permute-start | bytes 3145736 | tf_op jit(solution)/shard_map/ppermute | solution.py:240
  34.2 35.3 %collective-permute-start.3 = (bf16[128,64,128]{2,1,0:T(8,128)(2,1)}, bf16[128,64,128]{2,1,0:T(8,128)(2,1)}, u32[]{:S(2)}, u32[]{:S(2)}) collective-permute-start(bf16[128,64,128]{2,1,0:T(8,128)(2,1)} %pad_maximum_fusion.refs_0_), channel_id=1, source_target_pairs={{1,0},{0,1},{11,10},{10,11},{21,20},{20,21},{31,30},{30,31}} | collective-permute-start | bytes 6291464 | tf_op jit(solution)/shard_map/ppermute | solution.py:240
  37.0 11.0 %copy-start.6 = (s32[2]{0:T(128)S(1)}, s32[2]{0:T(128)}, u32[]{:S(2)}) copy-start(s32[2]{0:T(128)} %param.5) | copy-start | bytes 28
  37.3 26.9 %copy-start.2 = (bf16[128,64,128]{2,1,0:T(8,128)(2,1)}, bf16[128,64,128]{2,1,0:T(8,128)(2,1)S(1)}, u32[]{:S(2)}) copy-start(bf16[128,64,128]{2,1,0:T(8,128)(2,1)S(1)} %pad_maximum_fusion.1.refs_1_.refs_0_) | copy-start | bytes 6291460
  37.3 32.2 %collective-permute-start.6 = (bf16[128,64,128]{2,1,0:T(8,128)(2,1)S(1)}, bf16[128,64,128]{2,1,0:T(8,128)(2,1)}, u32[]{:S(2)}, u32[]{:S(2)}) collective-permute-start(bf16[128,64,128]{2,1,0:T(8,128)(2,1)S(1)} %pad_maximum_fusion.1.refs_1_.refs_0_), channel_id=1, source_target_pairs={{1,0},{0,1},{11,10},{10,11},{21,20},{20,21},{31,30},{30,31}} | collective-permute-start | bytes 6291464 | tf_op jit(solution)/shard_map/ppermute | solution.py:240
  41.3 28.3 %collective-permute-start.2 = (bf16[128,64,128]{2,1,0:T(8,128)(2,1)}, bf16[128,64,128]{2,1,0:T(8,128)(2,1)}, u32[]{:S(2)}, u32[]{:S(2)}) collective-permute-start(bf16[128,64,128]{2,1,0:T(8,128)(2,1)} %collective-permute-done.1.refs_1_), channel_id=1, source_target_pairs={{2,4},{3,5},{12,14},{13,15},{18,20},{19,21},{28,30},{29,31}} | collective-permute-start | bytes 6291464 | tf_op jit(solution)/shard_map/ppermute | solution.py:240
  43.3 27.3 %collective-permute-start.7 = (bf16[128,64,128]{2,1,0:T(8,128)(2,1)}, bf16[128,64,128]{2,1,0:T(8,128)(2,1)}, u32[]{:S(2)}, u32[]{:S(2)}) collective-permute-start(bf16[128,64,128]{2,1,0:T(8,128)(2,1)} %collective-permute-done.1.refs_1_), channel_id=1, source_target_pairs={{18,2},{19,3},{28,12},{29,13},{6,22},{7,23}} | collective-permute-start | bytes 6291464 | tf_op jit(solution)/shard_map/ppermute | solution.py:240
  64.2 3.3 %copy-start = (bf16[64,256,256]{2,1,0:T(8,128)(2,1)}, bf16[64,256,256]{2,1,0:T(8,128)(2,1)S(1)}, u32[]{:S(2)}) copy-start(bf16[64,256,256]{2,1,0:T(8,128)(2,1)S(1)} %get-tuple-element.26.refs_4_) | copy-start | bytes 25165828
  67.5 5.9 %collective-permute-start.10 = (bf16[128,64,128]{2,1,0:T(8,128)(2,1)}, bf16[128,64,128]{2,1,0:T(8,128)(2,1)}, u32[]{:S(2)}, u32[]{:S(2)}) collective-permute-start(bf16[128,64,128]{2,1,0:T(8,128)(2,1)} %collective-permute-done.1.refs_1_), channel_id=1, source_target_pairs={{3,2},{2,3},{13,12},{12,13},{23,22},{22,23}} | collective-permute-start | bytes 6291464 | tf_op jit(solution)/shard_map/ppermute | solution.py:240
  70.5 2.9 %collective-permute-start.11 = (bf16[128,64,128]{2,1,0:T(8,128)(2,1)}, bf16[128,64,128]{2,1,0:T(8,128)(2,1)S(1)}, u32[]{:S(2)}, u32[]{:S(2)}) collective-permute-start(bf16[128,64,128]{2,1,0:T(8,128)(2,1)} %collective-permute-done.2.refs_2_), channel_id=1, source_target_pairs={{5,4},{4,5},{15,14},{14,15}} | collective-permute-start | bytes 6291464 | tf_op jit(solution)/shard_map/ppermute | solution.py:240
  71.3 2.1 collective-permute-start.12
  72.1 28.2 %collective-permute-start.9 = (bf16[128,64,128]{2,1,0:T(8,128)(2,1)}, bf16[128,64,128]{2,1,0:T(8,128)(2,1)}, u32[]{:S(2)}, u32[]{:S(2)}) collective-permute-start(bf16[128,64,128]{2,1,0:T(8,128)(2,1)} %collective-permute-done.2.refs_2_), channel_id=1, source_target_pairs={{4,6},{5,7},{20,22},{21,23}} | collective-permute-start | bytes 6291464 | tf_op jit(solution)/shard_map/ppermute | solution.py:240
  73.5 1.3 copy-start.4
  74.7 51.5 %copy-start.3 = (bf16[128,64,128]{2,1,0:T(8,128)(2,1)}, bf16[128,64,128]{2,1,0:T(8,128)(2,1)S(1)}, u32[]{:S(2)}) copy-start(bf16[128,64,128]{2,1,0:T(8,128)(2,1)S(1)} %collective-permute-done.12.refs_2_) | copy-start | bytes 6291460
  100.4 70.9 %collective-permute-start.14 = (bf16[128,64,128]{2,1,0:T(8,128)(2,1)}, bf16[128,64,128]{2,1,0:T(8,128)(2,1)}, u32[]{:S(2)}, u32[]{:S(2)}) collective-permute-start(bf16[128,64,128]{2,1,0:T(8,128)(2,1)} %collective-permute-done.9.refs_3_), channel_id=1, source_target_pairs={{22,6},{23,7}} | collective-permute-start | bytes 6291464 | tf_op jit(solution)/shard_map/ppermute | solution.py:240
  101.7 74.0 %collective-permute-start.16 = (bf16[128,64,128]{2,1,0:T(8,128)(2,1)}, bf16[128,64,128]{2,1,0:T(8,128)(2,1)}, u32[]{:S(2)}, u32[]{:S(2)}) collective-permute-start(bf16[128,64,128]{2,1,0:T(8,128)(2,1)} %collective-permute-done.9.refs_3_), channel_id=1, source_target_pairs={{7,6},{6,7}} | collective-permute-start | bytes 6291464 | tf_op jit(solution)/shard_map/ppermute | solution.py:240
  105.4 103.9 %collective-permute-start.8 = (bf16[128,64,128]{2,1,0:T(8,128)(2,1)}, bf16[128,64,128]{2,1,0:T(8,128)(2,1)}, u32[]{:S(2)}, u32[]{:S(2)}) collective-permute-start(bf16[128,64,128]{2,1,0:T(8,128)(2,1)} %collective-permute-done.7.refs_1_), channel_id=1, source_target_pairs={{3,2},{2,3},{13,12},{12,13},{23,22},{22,23}} | collective-permute-start | bytes 6291464 | tf_op jit(solution)/shard_map/ppermute | solution.py:240
  107.4 101.9 %collective-permute-start.13 = (bf16[128,64,128]{2,1,0:T(8,128)(2,1)}, bf16[128,64,128]{2,1,0:T(8,128)(2,1)}, u32[]{:S(2)}, u32[]{:S(2)}) collective-permute-start(bf16[128,64,128]{2,1,0:T(8,128)(2,1)} %collective-permute-done.2.refs_2_), channel_id=1, source_target_pairs={{21,4},{20,5},{31,14},{30,15}} | collective-permute-start | bytes 6291464 | tf_op jit(solution)/shard_map/ppermute | solution.py:240
  171.3 38.1 %collective-permute-start.15 = (bf16[128,64,128]{2,1,0:T(8,128)(2,1)}, bf16[128,64,128]{2,1,0:T(8,128)(2,1)S(1)}, u32[]{:S(2)}, u32[]{:S(2)}) collective-permute-start(bf16[128,64,128]{2,1,0:T(8,128)(2,1)} %collective-permute-done.14.refs_3_), channel_id=1, source_target_pairs={{7,6},{6,7}} | collective-permute-start | bytes 6291464 | tf_op jit(solution)/shard_map/ppermute | solution.py:240
  209.4 1.3 copy-start.5

commit v2 on v1

--- a/solution.py
+++ b/solution.py
@@ -271,16 +271,18 @@
     after = lax.optimization_barrier
     once = climb(joined, 1)
     side_zero = to_row(joined, 0, 1, 0)
-    both_zero = to_row(joined_across, 0, 1, 0)
+    both_zero = to_row(joined, 0, 1, 1)
     twice = climb(once, 2)
     chip_one = to_row(once, 1, 0, 1)
     side_one = to_row(once, 1, 1, 0)
-    twice, side_zero, both_zero, chip_one, right, table = after((twice, side_zero, both_zero, chip_one, right, table))
+    twice, side_zero, both_zero, right, table = after((twice, side_zero, both_zero, right, table))
     thrice = climb(twice, 3)
     chip_two = to_row(twice, 2, 0, 1)
     side_two = to_row(twice, 2, 1, 0)
+    thrice, chip_one, side_one, chip_two, side_two, twice = after(
+        (thrice, chip_one, side_one, chip_two, side_two, twice)
+    )
     both_one = to_row(chip_one, 1, 1, 0)
-    thrice, side_one, side_two, chip_two, twice = after((thrice, side_one, side_two, chip_two, twice))
     chip_three = to_row(thrice, 3, 0, 1)
     side_three = to_row(thrice, 3, 1, 0)
     both_two = to_row(twice, 2, 1, 1)

time: 228 us -> 227 us (level)
  starting transfers between devices: 28.8 us -> 32.2 us
  waiting for transfers between devices: 95.2 us -> 92 us
    ppermute x17, starting transfers between devices: 28.8 us -> 32.2 us  [send(): return lax.ppermute(value, axes, number)]
    ppermute x17, waiting for transfers between devices: 95.2 us -> 92 us  [send(): return lax.ppermute(value, axes, number)]
    unnamed x14 -> x16, local copies, waits for them, and re-layouts: 7.51 us -> 7.5 us
  transfers between devices with their start and end apart: 17 -> 17, of which waited for: 7 -> 6; matrix products, arithmetic and copies ran while one was open for 5% -> 4% of each run, Pallas kernels for 26% -> 26%
where the time goes in v2:
time: 227 us; the launch traced here: 226 us
  waiting for transfers between devices  92 us (41%)
  Pallas kernels  82.9 us (37%)
  starting transfers between devices  32.2 us (14%)
  other arithmetic  9.84 us (4%)
  local copies, waits for them, and re-layouts  8.09 us (4%)
    ppermute x17, waiting for transfers between devices, send(): return lax.ppermute(value, axes, number)  92 us
    pallas_call x4, Pallas kernels, pair_block(): pl.pallas_call(functools.partial(pair_kernel, count=count, height=height,...  67 us
    ppermute x17, starting transfers between devices, send(): return lax.ppermute(value, axes, number)  32.2 us
    pallas_call x1, Pallas kernels, weights(): pl.pallas_call(functools.partial(weights_kernel, count=count, step=step),...  8.96 us
    unnamed x16, local copies, waits for them, and re-layouts  7.5 us
    pallas_call x1, Pallas kernels, whiten(): pl.pallas_call(functools.partial(whiten_kernel, width=width, parts=parts)...  6.96 us
  transfers between devices with their start and end apart: 17, of which 6 were waited for; matrix products, arithmetic and copies ran while one was open for 4% of the time, Pallas kernels for 26%

profile of v2, /device:TPU:26, one launch (start us, length us, event | category | flops | bytes accessed | tf_op | source)
XLA Modules:
  0.0 226.2 jit_solution(8463104825861324008)
XLA Ops:
  0.0 1.6 copy-done.1
  1.6 7.0 %whiten.1 = bf16[128,32,128]{2,1,0:T(8,128)(2,1)S(1)} custom-call(f32[1024,512]{1,0:T(8,128)S(1)} %bitcast.12, f32[1024,512]{1,0:T(8,128)S(1)} %bitcast.13, f32[1024,512]{1,0:T(8,128)S(1)} %bitcast.14, f32[1024,512]{1,0:T(8,128)S(1)} %bitcast.15), custom_call_target="tpu_custom_call" | custom-call | tf_op jit(solution)/shard_map/whiten/pallas_call | solution.py:51
  8.6 0.1 collective-permute-start
  8.7 2.6 %collective-permute-done = bf16[128,32,128]{2,1,0:T(8,128)(2,1)S(1)} collective-permute-done((bf16[128,32,128]{2,1,0:T(8,128)(2,1)S(1)}, bf16[128,32,128]{2,1,0:T(8,128)(2,1)S(1)}, u32[]{:S(2)}, u32[]{:S(2)}) %collective-permute-start) | collective-permute-done | bytes 1048608 | tf_op jit(solution)/shard_map/ppermute | solution.py:240
  11.3 0.1 broadcast_select_fusion.3
  11.4 0.0 copy-start.7
  11.4 0.3 pad_maximum_fusion.refs_0_
  11.7 0.0 copy-start.2
  11.7 1.3 collective-permute-start.1
  13.0 1.6 collective-permute-start.5
  14.6 2.0 collective-permute-start.4
  16.6 2.0 collective-permute-start.3
  18.6 21.2 %collective-permute-done.1.refs_1_ = bf16[128,64,128]{2,1,0:T(8,128)(2,1)} collective-permute-done((bf16[128,64,128]{2,1,0:T(8,128)(2,1)S(1)}, bf16[128,64,128]{2,1,0:T(8,128)(2,1)}, u32[]{:S(2)}, u32[]{:S(2)}) %collective-permute-start.1) | collective-permute-done | bytes 2097184 | tf_op jit(solution)/shard_map/ppermute | solution.py:240
  39.7 2.0 collective-permute-start.2
  41.8 18.6 %collective-permute-done.5 = bf16[128,32,128]{2,1,0:T(8,128)(2,1)} collective-permute-done((bf16[128,32,128]{2,1,0:T(8,128)(2,1)S(1)}, bf16[128,32,128]{2,1,0:T(8,128)(2,1)}, u32[]{:S(2)}, u32[]{:S(2)}) %collective-permute-start.5) | collective-permute-done | bytes 1048608 | tf_op jit(solution)/shard_map/ppermute | solution.py:240
  60.4 0.0 collective-permute-start.6
  60.4 0.1 pad_add_fusion.1.offset_ref
  60.5 0.0 copy-done.7
  60.5 0.6 fusion.15
  61.1 1.2 fusion.14
  62.3 1.2 and_convert_fusion
  63.5 2.0 multiply_convert_fusion.1
  65.5 0.8 pad_maximum_fusion.2.refs_5_
  66.3 0.0 collective-permute-done.6
  66.3 1.4 broadcast_select_fusion.1
  67.7 0.3 pad_maximum_fusion.1.refs_1_.refs_0_
  68.0 0.0 copy-done.2
  68.0 0.0 copy-start.3
  68.0 9.0 %weights.1 = (bf16[64,256,256]{2,1,0:T(8,128)(2,1)S(1)}, bf16[201,256,128]{2,1,0:T(8,128)(2,1)}) custom-call(s32[2]{0:T(128)S(1)} %pad_add_fusion.1.offset_ref, bf16[128,64,128]{2,1,0:T(8,128)(2,1)S(1)} %pad_maximum_fusion.refs_0_, bf16[128,64,128]{2,1,0:T(8,128)(2,1)S(1)} %pad_maximum_fusion.1.refs_1_.refs_0_), custom_call_target="tpu_custom_call" | custom-call | tf_op jit(solution)/shard_map/weights/pallas_call | solution.py:89
  77.0 0.0 copy-done.3
  77.0 3.3 %copy-done = bf16[64,256,256]{2,1,0:T(8,128)(2,1)} copy-done((bf16[64,256,256]{2,1,0:T(8,128)(2,1)}, bf16[64,256,256]{2,1,0:T(8,128)(2,1)S(1)}, u32[]{:S(2)}) %copy-start) | copy-done | bytes 8388632
  80.3 2.0 collective-permute-start.9
  82.3 6.3 %collective-permute-start.8 = (bf16[128,64,128]{2,1,0:T(8,128)(2,1)}, bf16[128,64,128]{2,1,0:T(8,128)(2,1)}, u32[]{:S(2)}, u32[]{:S(2)}) collective-permute-start(bf16[128,64,128]{2,1,0:T(8,128)(2,1)} %collective-permute-done.1.refs_1_), channel_id=1, source_target_pairs={{18,2},{19,3},{28,12},{29,13},{6,22},{7,23}} | collective-permute-start | bytes 6291464 | tf_op jit(solution)/shard_map/ppermute | solution.py:240
  88.5 0.0 collective-permute-done.4.refs_0_
  88.5 0.0 collective-permute-done.3.refs_0_
  88.5 0.0 collective-permute-done.2.refs_2_
  88.5 0.8 collective-permute-start.11
  89.3 0.8 collective-permute-start.10
  90.1 1.3 collective-permute-start.7
  91.4 0.0 collective-permute-done.9.refs_1_
  91.4 19.6 %collective-permute-done.8.refs_1_ = bf16[128,64,128]{2,1,0:T(8,128)(2,1)} collective-permute-done((bf16[128,64,128]{2,1,0:T(8,128)(2,1)}, bf16[128,64,128]{2,1,0:T(8,128)(2,1)}, u32[]{:S(2)}, u32[]{:S(2)}) %collective-permute-start.8) | collective-permute-done | bytes 2097184 | tf_op jit(solution)/shard_map/ppermute | solution.py:240
  111.0 0.0 collective-permute-done.11.refs_2_
  111.0 0.0 collective-permute-done.10.refs_2_
  111.1 1.3 copy-done.5
  112.3 6.0 %collective-permute-done.7.refs_3_ = bf16[128,64,128]{2,1,0:T(8,128)(2,1)} collective-permute-done((bf16[128,64,128]{2,1,0:T(8,128)(2,1)}, bf16[128,64,128]{2,1,0:T(8,128)(2,1)}, u32[]{:S(2)}, u32[]{:S(2)}) %collective-permute-start.7) | collective-permute-done | bytes 2097184 | tf_op jit(solution)/shard_map/ppermute | solution.py:240
  118.4 1.3 collective-permute-start.14
  119.7 3.4 %collective-permute-start.16 = (bf16[128,64,128]{2,1,0:T(8,128)(2,1)}, bf16[128,64,128]{2,1,0:T(8,128)(2,1)}, u32[]{:S(2)}, u32[]{:S(2)}) collective-permute-start(bf16[128,64,128]{2,1,0:T(8,128)(2,1)} %collective-permute-done.7.refs_3_), channel_id=1, source_target_pairs={{7,6},{6,7}} | collective-permute-start | bytes 6291464 | tf_op jit(solution)/shard_map/ppermute | solution.py:240
  123.7 0.7 pad_add_fusion.2.meta_ref
  124.4 2.0 collective-permute-start.12
  126.4 2.1 collective-permute-start.13
  128.5 16.7 %pair_block.4.refs_6_ = bf16[201,256,128]{2,1,0:T(8,128)(2,1)} custom-call(s32[2]{0:T(128)} %pad_add_fusion.2.meta_ref, bf16[128,64,128]{2,1,0:T(8,128)(2,1)} %copy-done.2, bf16[128,64,128]{2,1,0:T(8,128)(2,1)} %collective-permute-done.1.refs_1_, bf16[128,64,128]{2,1,0:T(8,128)(2,1)} %collective-permute-done.2.refs_2_, ...), custom_call_target="tpu_custom_call", output_to_operand_aliasing={{}: (7, {})} | custom-call | flops 7784628224 | bytes 11681792 | tf_op jit(solution)/shard_map/pair_block/pallas_call | solution.py:182
  145.2 23.9 %collective-permute-done.14.refs_3_ = bf16[128,64,128]{2,1,0:T(8,128)(2,1)} collective-permute-done((bf16[128,64,128]{2,1,0:T(8,128)(2,1)}, bf16[128,64,128]{2,1,0:T(8,128)(2,1)}, u32[]{:S(2)}, u32[]{:S(2)}) %collective-permute-start.14) | collective-permute-done | bytes 2097184 | tf_op jit(solution)/shard_map/ppermute | solution.py:240
  169.1 3.4 %collective-permute-start.15 = (bf16[128,64,128]{2,1,0:T(8,128)(2,1)}, bf16[128,64,128]{2,1,0:T(8,128)(2,1)S(1)}, u32[]{:S(2)}, u32[]{:S(2)}) collective-permute-start(bf16[128,64,128]{2,1,0:T(8,128)(2,1)} %collective-permute-done.14.refs_3_), channel_id=1, source_target_pairs={{7,6},{6,7}} | collective-permute-start | bytes 6291464 | tf_op jit(solution)/shard_map/ppermute | solution.py:240
  172.5 0.6 pad_add_fusion.3.meta_ref
  173.1 0.6 pad_add_fusion.4.meta_ref
  173.7 0.6 pad_add_fusion.meta_ref
  174.3 0.0 collective-permute-done.16.refs_3_
  174.3 16.7 %pair_block.5.refs_6_ = bf16[201,256,128]{2,1,0:T(8,128)(2,1)} custom-call(s32[2]{0:T(128)} %pad_add_fusion.4.meta_ref, bf16[128,64,128]{2,1,0:T(8,128)(2,1)} %collective-permute-done.3.refs_0_, bf16[128,64,128]{2,1,0:T(8,128)(2,1)} %collective-permute-done.9.refs_1_, bf16[128,64,128]{2,1,0:T(8,128)(2,1)} %copy-done.5, ...), custom_call_target="tpu_custom_call", output_to_operand_aliasing={{}: (7, {})} | custom-call | flops 7784628224 | bytes 11681792 | tf_op jit(solution)/shard_map/pair_block/pallas_call | solution.py:182
  191.0 16.9 %pair_block.6.refs_6_ = bf16[201,256,128]{2,1,0:T(8,128)(2,1)} custom-call(s32[2]{0:T(128)} %pad_add_fusion.3.meta_ref, bf16[128,64,128]{2,1,0:T(8,128)(2,1)} %copy-done.3, bf16[128,64,128]{2,1,0:T(8,128)(2,1)} %collective-permute-done.8.refs_1_, bf16[128,64,128]{2,1,0:T(8,128)(2,1)} %copy-done.4, ...), custom_call_target="tpu_custom_call", output_to_operand_aliasing={{}: (7, {})} | custom-call | flops 7784628224 | bytes 11681792 | tf_op jit(solution)/shard_map/pair_block/pallas_call | solution.py:182
  207.9 0.0 collective-permute-done.12.refs_1_
  207.9 0.0 collective-permute-done.13.refs_2_
  208.0 0.0 collective-permute-done.15.refs_3_
  208.0 1.3 copy-done.6
  209.3 16.7 %pair_block.7 = bf16[201,256,128]{2,1,0:T(8,128)(2,1)} custom-call(s32[2]{0:T(128)} %pad_add_fusion.meta_ref, bf16[128,64,128]{2,1,0:T(8,128)(2,1)} %collective-permute-done.4.refs_0_, bf16[128,64,128]{2,1,0:T(8,128)(2,1)} %collective-permute-done.12.refs_1_, bf16[128,64,128]{2,1,0:T(8,128)(2,1)} %collective-permute-done.13.refs_2_, ...), custom_call_target="tpu_custom_call", output_to_operand_aliasing={{}: (7, {})} | custom-call | flops 7784628224 | bytes 11681792 | tf_op jit(solution)/shard_map/pair_block/pallas_call | solution.py:182
  (8 shorter events, 0.0 us)
Async XLA Ops:
  0.0 1.6 copy-start.1
  8.6 2.7 %collective-permute-start = (bf16[128,32,128]{2,1,0:T(8,128)(2,1)S(1)}, bf16[128,32,128]{2,1,0:T(8,128)(2,1)S(1)}, u32[]{:S(2)}, u32[]{:S(2)}) collective-permute-start(bf16[128,32,128]{2,1,0:T(8,128)(2,1)S(1)} %whiten.1), channel_id=1, source_target_pairs={{0,8},{1,9},{2,10},{3,11},{4,12},{5,13},{6,14},{7,15},{8,0},{9,1},... | collective-permute-start | bytes 3145736 | tf_op jit(solution)/shard_map/ppermute | solution.py:240
  11.4 49.0 %copy-start.7 = (s32[2]{0:T(128)S(1)}, s32[2]{0:T(128)}, u32[]{:S(2)}) copy-start(s32[2]{0:T(128)} %param.5) | copy-start | bytes 28
  11.7 56.3 %copy-start.2 = (bf16[128,64,128]{2,1,0:T(8,128)(2,1)}, bf16[128,64,128]{2,1,0:T(8,128)(2,1)S(1)}, u32[]{:S(2)}) copy-start(bf16[128,64,128]{2,1,0:T(8,128)(2,1)S(1)} %pad_maximum_fusion.refs_0_) | copy-start | bytes 6291460
  11.7 28.0 %collective-permute-start.1 = (bf16[128,64,128]{2,1,0:T(8,128)(2,1)S(1)}, bf16[128,64,128]{2,1,0:T(8,128)(2,1)}, u32[]{:S(2)}, u32[]{:S(2)}) collective-permute-start(bf16[128,64,128]{2,1,0:T(8,128)(2,1)S(1)} %pad_maximum_fusion.refs_0_), channel_id=1, source_target_pairs={{0,2},{1,3},{4,6},{5,7},{10,12},{11,13},{16,18},{17,19},{20,22},{2... | collective-permute-start | bytes 6291464 | tf_op jit(solution)/shard_map/ppermute | solution.py:240
  13.0 47.4 %collective-permute-start.5 = (bf16[128,32,128]{2,1,0:T(8,128)(2,1)S(1)}, bf16[128,32,128]{2,1,0:T(8,128)(2,1)}, u32[]{:S(2)}, u32[]{:S(2)}) collective-permute-start(bf16[128,32,128]{2,1,0:T(8,128)(2,1)S(1)} %whiten.1), channel_id=1, source_target_pairs={{0,16},{1,17},{2,18},{3,19},{4,20},{5,21},{6,22},{7,23},{8,24},{9,... | collective-permute-start | bytes 3145736 | tf_op jit(solution)/shard_map/ppermute | solution.py:240
  14.6 73.9 %collective-permute-start.4 = (bf16[128,64,128]{2,1,0:T(8,128)(2,1)S(1)}, bf16[128,64,128]{2,1,0:T(8,128)(2,1)}, u32[]{:S(2)}, u32[]{:S(2)}) collective-permute-start(bf16[128,64,128]{2,1,0:T(8,128)(2,1)S(1)} %pad_maximum_fusion.refs_0_), channel_id=1, source_target_pairs={{17,0},{16,1},{27,10},{26,11},{5,20},{4,21},{15,30},{14,31}} | collective-permute-start | bytes 6291464 | tf_op jit(solution)/shard_map/ppermute | solution.py:240
  16.6 71.9 %collective-permute-start.3 = (bf16[128,64,128]{2,1,0:T(8,128)(2,1)S(1)}, bf16[128,64,128]{2,1,0:T(8,128)(2,1)}, u32[]{:S(2)}, u32[]{:S(2)}) collective-permute-start(bf16[128,64,128]{2,1,0:T(8,128)(2,1)S(1)} %pad_maximum_fusion.refs_0_), channel_id=1, source_target_pairs={{1,0},{0,1},{11,10},{10,11},{21,20},{20,21},{31,30},{30,31}} | collective-permute-start | bytes 6291464 | tf_op jit(solution)/shard_map/ppermute | solution.py:240
  39.7 48.8 %collective-permute-start.2 = (bf16[128,64,128]{2,1,0:T(8,128)(2,1)}, bf16[128,64,128]{2,1,0:T(8,128)(2,1)}, u32[]{:S(2)}, u32[]{:S(2)}) collective-permute-start(bf16[128,64,128]{2,1,0:T(8,128)(2,1)} %collective-permute-done.1.refs_1_), channel_id=1, source_target_pairs={{2,4},{3,5},{12,14},{13,15},{18,20},{19,21},{28,30},{29,31}} | collective-permute-start | bytes 6291464 | tf_op jit(solution)/shard_map/ppermute | solution.py:240
  60.4 5.9 %collective-permute-start.6 = (bf16[128,32,128]{2,1,0:T(8,128)(2,1)}, bf16[128,32,128]{2,1,0:T(8,128)(2,1)S(1)}, u32[]{:S(2)}, u32[]{:S(2)}) collective-permute-start(bf16[128,32,128]{2,1,0:T(8,128)(2,1)} %collective-permute-done.5), channel_id=1, source_target_pairs={{0,8},{1,9},{2,10},{3,11},{4,12},{5,13},{6,14},{7,15},{8,0},{9,1},... | collective-permute-start | bytes 3145736 | tf_op jit(solution)/shard_map/ppermute | solution.py:240
  68.0 9.0 %copy-start.3 = (bf16[128,64,128]{2,1,0:T(8,128)(2,1)}, bf16[128,64,128]{2,1,0:T(8,128)(2,1)S(1)}, u32[]{:S(2)}) copy-start(bf16[128,64,128]{2,1,0:T(8,128)(2,1)S(1)} %pad_maximum_fusion.1.refs_1_.refs_0_) | copy-start | bytes 6291460
  77.0 3.3 %copy-start = (bf16[64,256,256]{2,1,0:T(8,128)(2,1)}, bf16[64,256,256]{2,1,0:T(8,128)(2,1)S(1)}, u32[]{:S(2)}) copy-start(bf16[64,256,256]{2,1,0:T(8,128)(2,1)S(1)} %get-tuple-element.26.refs_4_) | copy-start | bytes 25165828
  80.3 11.2 %collective-permute-start.9 = (bf16[128,64,128]{2,1,0:T(8,128)(2,1)}, bf16[128,64,128]{2,1,0:T(8,128)(2,1)}, u32[]{:S(2)}, u32[]{:S(2)}) collective-permute-start(bf16[128,64,128]{2,1,0:T(8,128)(2,1)} %collective-permute-done.1.refs_1_), channel_id=1, source_target_pairs={{3,2},{2,3},{13,12},{12,13},{23,22},{22,23}} | collective-permute-start | bytes 6291464 | tf_op jit(solution)/shard_map/ppermute | solution.py:240
  82.3 28.8 %collective-permute-start.8 = (bf16[128,64,128]{2,1,0:T(8,128)(2,1)}, bf16[128,64,128]{2,1,0:T(8,128)(2,1)}, u32[]{:S(2)}, u32[]{:S(2)}) collective-permute-start(bf16[128,64,128]{2,1,0:T(8,128)(2,1)} %collective-permute-done.1.refs_1_), channel_id=1, source_target_pairs={{18,2},{19,3},{28,12},{29,13},{6,22},{7,23}} | collective-permute-start | bytes 6291464 | tf_op jit(solution)/shard_map/ppermute | solution.py:240
  88.5 22.5 %collective-permute-start.11 = (bf16[128,64,128]{2,1,0:T(8,128)(2,1)}, bf16[128,64,128]{2,1,0:T(8,128)(2,1)S(1)}, u32[]{:S(2)}, u32[]{:S(2)}) collective-permute-start(bf16[128,64,128]{2,1,0:T(8,128)(2,1)} %collective-permute-done.2.refs_2_), channel_id=1, source_target_pairs={{5,4},{4,5},{15,14},{14,15}} | collective-permute-start | bytes 6291464 | tf_op jit(solution)/shard_map/ppermute | solution.py:240
  89.3 21.7 %collective-permute-start.10 = (bf16[128,64,128]{2,1,0:T(8,128)(2,1)}, bf16[128,64,128]{2,1,0:T(8,128)(2,1)S(1)}, u32[]{:S(2)}, u32[]{:S(2)}) collective-permute-start(bf16[128,64,128]{2,1,0:T(8,128)(2,1)} %collective-permute-done.2.refs_2_), channel_id=1, source_target_pairs={{20,4},{21,5},{30,14},{31,15}} | collective-permute-start | bytes 6291464 | tf_op jit(solution)/shard_map/ppermute | solution.py:240
  90.1 28.2 %collective-permute-start.7 = (bf16[128,64,128]{2,1,0:T(8,128)(2,1)}, bf16[128,64,128]{2,1,0:T(8,128)(2,1)}, u32[]{:S(2)}, u32[]{:S(2)}) collective-permute-start(bf16[128,64,128]{2,1,0:T(8,128)(2,1)} %collective-permute-done.2.refs_2_), channel_id=1, source_target_pairs={{4,6},{5,7},{20,22},{21,23}} | collective-permute-start | bytes 6291464 | tf_op jit(solution)/shard_map/ppermute | solution.py:240
  111.0 1.3 copy-start.5
  112.3 32.9 %copy-start.4 = (bf16[128,64,128]{2,1,0:T(8,128)(2,1)}, bf16[128,64,128]{2,1,0:T(8,128)(2,1)S(1)}, u32[]{:S(2)}) copy-start(bf16[128,64,128]{2,1,0:T(8,128)(2,1)S(1)} %collective-permute-done.10.refs_2_) | copy-start | bytes 6291460
  118.4 50.7 %collective-permute-start.14 = (bf16[128,64,128]{2,1,0:T(8,128)(2,1)}, bf16[128,64,128]{2,1,0:T(8,128)(2,1)}, u32[]{:S(2)}, u32[]{:S(2)}) collective-permute-start(bf16[128,64,128]{2,1,0:T(8,128)(2,1)} %collective-permute-done.7.refs_3_), channel_id=1, source_target_pairs={{22,6},{23,7}} | collective-permute-start | bytes 6291464 | tf_op jit(solution)/shard_map/ppermute | solution.py:240
  119.7 54.7 %collective-permute-start.16 = (bf16[128,64,128]{2,1,0:T(8,128)(2,1)}, bf16[128,64,128]{2,1,0:T(8,128)(2,1)}, u32[]{:S(2)}, u32[]{:S(2)}) collective-permute-start(bf16[128,64,128]{2,1,0:T(8,128)(2,1)} %collective-permute-done.7.refs_3_), channel_id=1, source_target_pairs={{7,6},{6,7}} | collective-permute-start | bytes 6291464 | tf_op jit(solution)/shard_map/ppermute | solution.py:240
  124.4 83.5 %collective-permute-start.12 = (bf16[128,64,128]{2,1,0:T(8,128)(2,1)}, bf16[128,64,128]{2,1,0:T(8,128)(2,1)}, u32[]{:S(2)}, u32[]{:S(2)}) collective-permute-start(bf16[128,64,128]{2,1,0:T(8,128)(2,1)} %collective-permute-done.8.refs_1_), channel_id=1, source_target_pairs={{3,2},{2,3},{13,12},{12,13},{23,22},{22,23}} | collective-permute-start | bytes 6291464 | tf_op jit(solution)/shard_map/ppermute | solution.py:240
  126.4 81.5 %collective-permute-start.13 = (bf16[128,64,128]{2,1,0:T(8,128)(2,1)}, bf16[128,64,128]{2,1,0:T(8,128)(2,1)}, u32[]{:S(2)}, u32[]{:S(2)}) collective-permute-start(bf16[128,64,128]{2,1,0:T(8,128)(2,1)} %collective-permute-done.2.refs_2_), channel_id=1, source_target_pairs={{21,4},{20,5},{31,14},{30,15}} | collective-permute-start | bytes 6291464 | tf_op jit(solution)/shard_map/ppermute | solution.py:240
  169.1 38.9 %collective-permute-start.15 = (bf16[128,64,128]{2,1,0:T(8,128)(2,1)}, bf16[128,64,128]{2,1,0:T(8,128)(2,1)S(1)}, u32[]{:S(2)}, u32[]{:S(2)}) collective-permute-start(bf16[128,64,128]{2,1,0:T(8,128)(2,1)} %collective-permute-done.14.refs_3_), channel_id=1, source_target_pairs={{7,6},{6,7}} | collective-permute-start | bytes 6291464 | tf_op jit(solution)/shard_map/ppermute | solution.py:240
  208.0 1.3 copy-start.6

commit v3 on v2

--- a/solution.py
+++ b/solution.py
@@ -250,10 +250,6 @@
     shard = whiten(spectra, 1)[0]
     joined = join(shard, send(shard, core_flip))
     across = send(shard, chip_flip)
-    joined_across = join(across, send(across, core_flip))
-    offsets = jnp.stack([2 * chip * width, 2 * (1 - chip) * width]).astype(jnp.int32)
-    right, out = weights(offsets, [joined, joined_across], sides * rows * width)
-
     def climb(value, d):
         return send(
             value,
@@ -272,20 +268,23 @@
     once = climb(joined, 1)
     side_zero = to_row(joined, 0, 1, 0)
     both_zero = to_row(joined, 0, 1, 1)
+    once, table, across = after((once, table, across))
     twice = climb(once, 2)
+    joined_across = join(across, send(across, core_flip))
+    offsets = jnp.stack([2 * chip * width, 2 * (1 - chip) * width]).astype(jnp.int32)
+    right, out = weights(offsets, [joined, joined_across], sides * rows * width)
     chip_one = to_row(once, 1, 0, 1)
     side_one = to_row(once, 1, 1, 0)
-    twice, side_zero, both_zero, right, table = after((twice, side_zero, both_zero, right, table))
+    twice, side_zero, both_zero = after((twice, side_zero, both_zero))
     thrice = climb(twice, 3)
     chip_two = to_row(twice, 2, 0, 1)
     side_two = to_row(twice, 2, 1, 0)
-    thrice, chip_one, side_one, chip_two, side_two, twice = after(
-        (thrice, chip_one, side_one, chip_two, side_two, twice)
+    thrice, chip_one, side_one, chip_two, side_two, twice, right, out = after(
+        (thrice, chip_one, side_one, chip_two, side_two, twice, right, out)
     )
     both_one = to_row(chip_one, 1, 1, 0)
     chip_three = to_row(thrice, 3, 0, 1)
     side_three = to_row(thrice, 3, 1, 0)
-    both_two = to_row(twice, 2, 1, 1)
 
     by_depth = jnp.where(request == 1, depth, -1)
 
@@ -293,7 +292,8 @@
         return ((side ^ flip_side) * rows + 2 * (chip ^ flip_chip)) * width
 
     out = pair_block(by_depth, place(0, 0), [joined, once, twice, thrice], right, table, out)
-    chip_three, out = after((chip_three, out))
+    chip_three, twice, out = after((chip_three, twice, out))
+    both_two = to_row(twice, 2, 1, 1)
     both_three = to_row(chip_three, 3, 1, 0)
     out = pair_block(by_depth, place(1, 0), [side_zero, side_one, side_two, side_three], right, table, out)
     out = pair_block(by_depth, place(0, 1), [joined_across, chip_one, chip_two, chip_three], right, table, out)

time: 227 us -> 204 us (0.90)
  waiting for transfers between devices: 92 us -> 70 us
    ppermute x17, waiting for transfers between devices: 92 us -> 70 us  [send(): return lax.ppermute(value, axes, number)]
    unnamed x16 -> x18, local copies, waits for them, and re-layouts: 7.5 us -> 6.25 us
  transfers between devices with their start and end apart: 17 -> 17, of which waited for: 6 -> 4; matrix products, arithmetic and copies ran while one was open for 4% -> 5% of each run, Pallas kernels for 26% -> 29%
where the time goes in v3:
time: 204 us; the launch traced here: 203 us
  Pallas kernels  83 us (41%)
  waiting for transfers between devices  70 us (34%)
  starting transfers between devices  31.6 us (15%)
  other arithmetic  10.1 us (5%)
  local copies, waits for them, and re-layouts  6.86 us (3%)
    ppermute x17, waiting for transfers between devices, send(): return lax.ppermute(value, axes, number)  70 us
    pallas_call x4, Pallas kernels, pair_block(): pl.pallas_call(functools.partial(pair_kernel, count=count, height=height,...  67 us
    ppermute x17, starting transfers between devices, send(): return lax.ppermute(value, axes, number)  31.6 us
    pallas_call x1, Pallas kernels, weights(): pl.pallas_call(functools.partial(weights_kernel, count=count, step=step),...  8.96 us
    pallas_call x1, Pallas kernels, whiten(): pl.pallas_call(functools.partial(whiten_kernel, width=width, parts=parts)...  6.96 us
    unnamed x18, local copies, waits for them, and re-layouts  6.25 us
  transfers between devices with their start and end apart: 17, of which 4 were waited for; matrix products, arithmetic and copies ran while one was open for 5% of the time, Pallas kernels for 29%

profile of v3, /device:TPU:26, one launch (start us, length us, event | category | flops | bytes accessed | tf_op | source)
XLA Modules:
  0.0 202.6 jit_solution(5191477590767519307)
XLA Ops:
  0.0 1.6 copy-done.1
  1.6 7.0 %whiten.1 = bf16[128,32,128]{2,1,0:T(8,128)(2,1)S(1)} custom-call(f32[1024,512]{1,0:T(8,128)S(1)} %bitcast.12, f32[1024,512]{1,0:T(8,128)S(1)} %bitcast.13, f32[1024,512]{1,0:T(8,128)S(1)} %bitcast.14, f32[1024,512]{1,0:T(8,128)S(1)} %bitcast.15), custom_call_target="tpu_custom_call" | custom-call | tf_op jit(solution)/shard_map/whiten/pallas_call | solution.py:51
  8.6 0.1 collective-permute-start
  8.7 2.6 %collective-permute-done = bf16[128,32,128]{2,1,0:T(8,128)(2,1)S(1)} collective-permute-done((bf16[128,32,128]{2,1,0:T(8,128)(2,1)S(1)}, bf16[128,32,128]{2,1,0:T(8,128)(2,1)S(1)}, u32[]{:S(2)}, u32[]{:S(2)}) %collective-permute-start) | collective-permute-done | bytes 1048608 | tf_op jit(solution)/shard_map/ppermute | solution.py:240
  11.3 0.1 broadcast_select_fusion.3
  11.4 0.0 copy-start.8
  11.4 0.3 pad_maximum_fusion.refs_0_
  11.7 0.0 copy-start.2
  11.7 1.3 collective-permute-start.1
  13.0 1.6 collective-permute-start.2
  14.6 0.0 copy-done.8
  14.6 0.6 fusion.15
  15.2 1.3 and_convert_fusion
  16.5 1.3 fusion.14
  17.8 2.0 multiply_convert_fusion.1
  19.8 0.8 pad_maximum_fusion.2.refs_5_
  20.6 0.8 collective-permute-start.4
  21.4 0.8 collective-permute-start.5
  22.2 38.2 %collective-permute-done.2 = bf16[128,32,128]{2,1,0:T(8,128)(2,1)S(1)} collective-permute-done((bf16[128,32,128]{2,1,0:T(8,128)(2,1)S(1)}, bf16[128,32,128]{2,1,0:T(8,128)(2,1)S(1)}, u32[]{:S(2)}, u32[]{:S(2)}) %collective-permute-start.2) | collective-permute-done | bytes 1048608 | tf_op jit(solution)/shard_map/ppermute | solution.py:240
  60.4 0.0 collective-permute-done.1.refs_1_
  60.4 2.0 %collective-permute-start.3 = (bf16[128,64,128]{2,1,0:T(8,128)(2,1)}, bf16[128,64,128]{2,1,0:T(8,128)(2,1)}, u32[]{:S(2)}, u32[]{:S(2)}) collective-permute-start(bf16[128,64,128]{2,1,0:T(8,128)(2,1)} %collective-permute-done.1.refs_1_), channel_id=1, source_target_pairs={{2,4},{3,5},{12,14},{13,15},{18,20},{19,21},{28,30},{29,31}} | collective-permute-start | bytes 6291464 | tf_op jit(solution)/shard_map/ppermute | solution.py:240
  62.4 0.0 collective-permute-start.11
  62.5 5.7 %collective-permute-start.7 = (bf16[128,64,128]{2,1,0:T(8,128)(2,1)}, bf16[128,64,128]{2,1,0:T(8,128)(2,1)}, u32[]{:S(2)}, u32[]{:S(2)}) collective-permute-start(bf16[128,64,128]{2,1,0:T(8,128)(2,1)} %collective-permute-done.1.refs_1_), channel_id=1, source_target_pairs={{18,2},{19,3},{28,12},{29,13},{6,22},{7,23}} | collective-permute-start | bytes 6291464 | tf_op jit(solution)/shard_map/ppermute | solution.py:240
  68.1 0.0 collective-permute-done.4.refs_0_
  68.2 2.0 collective-permute-start.8
  70.1 0.0 collective-permute-done.5.refs_0_
  70.1 1.4 copy-done.4
  71.5 0.0 collective-permute-done.3.refs_2_
  71.5 0.0 copy-done.5
  71.5 2.0 collective-permute-start.10
  73.5 0.0 copy-done.7
  73.5 1.3 collective-permute-start.6
  74.8 0.0 collective-permute-done.11
  74.8 2.0 collective-permute-start.9
  76.8 0.1 pad_add_fusion.1.offset_ref
  76.9 1.4 broadcast_select_fusion.1
  78.2 0.3 pad_maximum_fusion.1.refs_1_.refs_0_
  78.5 0.0 copy-done.2
  78.6 9.0 %weights.1 = (bf16[64,256,256]{2,1,0:T(8,128)(2,1)S(1)}, bf16[201,256,128]{2,1,0:T(8,128)(2,1)}) custom-call(s32[2]{0:T(128)S(1)} %pad_add_fusion.1.offset_ref, bf16[128,64,128]{2,1,0:T(8,128)(2,1)S(1)} %pad_maximum_fusion.refs_0_, bf16[128,64,128]{2,1,0:T(8,128)(2,1)S(1)} %pad_maximum_fusion.1.refs_1_.refs_0_), custom_call_target="tpu_custom_call" | custom-call | tf_op jit(solution)/shard_map/weights/pallas_call | solution.py:89
  87.5 0.0 copy-done.3
  87.5 3.3 %copy-done = bf16[64,256,256]{2,1,0:T(8,128)(2,1)} copy-done((bf16[64,256,256]{2,1,0:T(8,128)(2,1)}, bf16[64,256,256]{2,1,0:T(8,128)(2,1)S(1)}, u32[]{:S(2)}) %copy-start) | copy-done | bytes 8388632
  90.8 0.0 collective-permute-done.7.refs_1_
  90.8 0.0 collective-permute-done.8.refs_1_
  90.8 0.0 collective-permute-done.10.refs_2_
  90.8 25.7 %collective-permute-done.6.refs_3_ = bf16[128,64,128]{2,1,0:T(8,128)(2,1)} collective-permute-done((bf16[128,64,128]{2,1,0:T(8,128)(2,1)}, bf16[128,64,128]{2,1,0:T(8,128)(2,1)}, u32[]{:S(2)}, u32[]{:S(2)}) %collective-permute-start.6) | collective-permute-done | bytes 2097184 | tf_op jit(solution)/shard_map/ppermute | solution.py:240
  116.5 0.0 collective-permute-done.9.refs_2_
  116.5 1.3 collective-permute-start.13
  117.8 3.4 %collective-permute-start.16 = (bf16[128,64,128]{2,1,0:T(8,128)(2,1)}, bf16[128,64,128]{2,1,0:T(8,128)(2,1)}, u32[]{:S(2)}, u32[]{:S(2)}) collective-permute-start(bf16[128,64,128]{2,1,0:T(8,128)(2,1)} %collective-permute-done.6.refs_3_), channel_id=1, source_target_pairs={{7,6},{6,7}} | collective-permute-start | bytes 6291464 | tf_op jit(solution)/shard_map/ppermute | solution.py:240
  121.9 0.6 pad_add_fusion.2.meta_ref
  122.6 2.0 %collective-permute-start.12 = (bf16[128,64,128]{2,1,0:T(8,128)(2,1)}, bf16[128,64,128]{2,1,0:T(8,128)(2,1)}, u32[]{:S(2)}, u32[]{:S(2)}) collective-permute-start(bf16[128,64,128]{2,1,0:T(8,128)(2,1)} %collective-permute-done.7.refs_1_), channel_id=1, source_target_pairs={{3,2},{2,3},{13,12},{12,13},{23,22},{22,23}} | collective-permute-start | bytes 6291464 | tf_op jit(solution)/shard_map/ppermute | solution.py:240
  124.6 16.7 %pair_block.4.refs_6_ = bf16[201,256,128]{2,1,0:T(8,128)(2,1)} custom-call(s32[2]{0:T(128)} %pad_add_fusion.2.meta_ref, bf16[128,64,128]{2,1,0:T(8,128)(2,1)} %copy-done.2, bf16[128,64,128]{2,1,0:T(8,128)(2,1)} %collective-permute-done.1.refs_1_, bf16[128,64,128]{2,1,0:T(8,128)(2,1)} %collective-permute-done.3.refs_2_, ...), custom_call_target="tpu_custom_call", output_to_operand_aliasing={{}: (7, {})} | custom-call | flops 7784628224 | bytes 11681792 | tf_op jit(solution)/shard_map/pair_block/pallas_call | solution.py:182
  141.3 3.4 %collective-permute-done.13.refs_3_ = bf16[128,64,128]{2,1,0:T(8,128)(2,1)S(1)} collective-permute-done((bf16[128,64,128]{2,1,0:T(8,128)(2,1)}, bf16[128,64,128]{2,1,0:T(8,128)(2,1)S(1)}, u32[]{:S(2)}, u32[]{:S(2)}) %collective-permute-start.13) | collective-permute-done | bytes 2097184 | tf_op jit(solution)/shard_map/ppermute | solution.py:240
  144.7 2.0 collective-permute-start.14
  146.6 3.4 %collective-permute-start.15 = (bf16[128,64,128]{2,1,0:T(8,128)(2,1)S(1)}, bf16[128,64,128]{2,1,0:T(8,128)(2,1)}, u32[]{:S(2)}, u32[]{:S(2)}) collective-permute-start(bf16[128,64,128]{2,1,0:T(8,128)(2,1)S(1)} %collective-permute-done.13.refs_3_), channel_id=1, source_target_pairs={{7,6},{6,7}} | collective-permute-start | bytes 6291464 | tf_op jit(solution)/shard_map/ppermute | solution.py:240
  150.1 0.7 pad_add_fusion.4.meta_ref
  150.7 0.7 pad_add_fusion.3.meta_ref
  151.4 0.6 pad_add_fusion.meta_ref
  152.0 0.0 collective-permute-done.16.refs_3_
  152.0 16.7 %pair_block.5.refs_6_ = bf16[201,256,128]{2,1,0:T(8,128)(2,1)} custom-call(s32[2]{0:T(128)} %pad_add_fusion.4.meta_ref, bf16[128,64,128]{2,1,0:T(8,128)(2,1)} %copy-done.5, bf16[128,64,128]{2,1,0:T(8,128)(2,1)} %collective-permute-done.8.refs_1_, bf16[128,64,128]{2,1,0:T(8,128)(2,1)} %collective-permute-done.10.refs_2_, ...), custom_call_target="tpu_custom_call", output_to_operand_aliasing={{}: (7, {})} | custom-call | flops 7784628224 | bytes 11681792 | tf_op jit(solution)/shard_map/pair_block/pallas_call | solution.py:182
  168.7 16.9 %pair_block.6.refs_6_ = bf16[201,256,128]{2,1,0:T(8,128)(2,1)} custom-call(s32[2]{0:T(128)} %pad_add_fusion.3.meta_ref, bf16[128,64,128]{2,1,0:T(8,128)(2,1)} %copy-done.3, bf16[128,64,128]{2,1,0:T(8,128)(2,1)} %collective-permute-done.7.refs_1_, bf16[128,64,128]{2,1,0:T(8,128)(2,1)} %collective-permute-done.9.refs_2_, ...), custom_call_target="tpu_custom_call", output_to_operand_aliasing={{}: (7, {})} | custom-call | flops 7784628224 | bytes 11681792 | tf_op jit(solution)/shard_map/pair_block/pallas_call | solution.py:182
  185.7 0.0 collective-permute-done.12.refs_1_
  185.7 0.0 collective-permute-done.14.refs_2_
  185.7 0.0 collective-permute-done.15.refs_3_
  185.7 16.7 %pair_block.7 = bf16[201,256,128]{2,1,0:T(8,128)(2,1)} custom-call(s32[2]{0:T(128)} %pad_add_fusion.meta_ref, bf16[128,64,128]{2,1,0:T(8,128)(2,1)} %copy-done.4, bf16[128,64,128]{2,1,0:T(8,128)(2,1)} %collective-permute-done.12.refs_1_, bf16[128,64,128]{2,1,0:T(8,128)(2,1)} %collective-permute-done.14.refs_2_, ...), custom_call_target="tpu_custom_call", output_to_operand_aliasing={{}: (7, {})} | custom-call | flops 7784628224 | bytes 11681792 | tf_op jit(solution)/shard_map/pair_block/pallas_call | solution.py:182
  (10 shorter events, 0.0 us)
Async XLA Ops:
  0.0 1.6 copy-start.1
  8.6 2.7 %collective-permute-start = (bf16[128,32,128]{2,1,0:T(8,128)(2,1)S(1)}, bf16[128,32,128]{2,1,0:T(8,128)(2,1)S(1)}, u32[]{:S(2)}, u32[]{:S(2)}) collective-permute-start(bf16[128,32,128]{2,1,0:T(8,128)(2,1)S(1)} %whiten.1), channel_id=1, source_target_pairs={{0,8},{1,9},{2,10},{3,11},{4,12},{5,13},{6,14},{7,15},{8,0},{9,1},... | collective-permute-start | bytes 3145736 | tf_op jit(solution)/shard_map/ppermute | solution.py:240
  11.4 3.2 %copy-start.8 = (s32[2]{0:T(128)S(1)}, s32[2]{0:T(128)}, u32[]{:S(2)}) copy-start(s32[2]{0:T(128)} %param.5) | copy-start | bytes 28
  11.7 66.8 %copy-start.2 = (bf16[128,64,128]{2,1,0:T(8,128)(2,1)}, bf16[128,64,128]{2,1,0:T(8,128)(2,1)S(1)}, u32[]{:S(2)}) copy-start(bf16[128,64,128]{2,1,0:T(8,128)(2,1)S(1)} %pad_maximum_fusion.refs_0_) | copy-start | bytes 6291460
  11.7 48.7 %collective-permute-start.1 = (bf16[128,64,128]{2,1,0:T(8,128)(2,1)S(1)}, bf16[128,64,128]{2,1,0:T(8,128)(2,1)}, u32[]{:S(2)}, u32[]{:S(2)}) collective-permute-start(bf16[128,64,128]{2,1,0:T(8,128)(2,1)S(1)} %pad_maximum_fusion.refs_0_), channel_id=1, source_target_pairs={{0,2},{1,3},{4,6},{5,7},{10,12},{11,13},{16,18},{17,19},{20,22},{2... | collective-permute-start | bytes 6291464 | tf_op jit(solution)/shard_map/ppermute | solution.py:240
  13.0 47.4 %collective-permute-start.2 = (bf16[128,32,128]{2,1,0:T(8,128)(2,1)S(1)}, bf16[128,32,128]{2,1,0:T(8,128)(2,1)S(1)}, u32[]{:S(2)}, u32[]{:S(2)}) collective-permute-start(bf16[128,32,128]{2,1,0:T(8,128)(2,1)S(1)} %whiten.1), channel_id=1, source_target_pairs={{0,16},{1,17},{2,18},{3,19},{4,20},{5,21},{6,22},{7,23},{8,24},{9,... | collective-permute-start | bytes 3145736 | tf_op jit(solution)/shard_map/ppermute | solution.py:240
  20.6 47.6 %collective-permute-start.4 = (bf16[128,64,128]{2,1,0:T(8,128)(2,1)S(1)}, bf16[128,64,128]{2,1,0:T(8,128)(2,1)S(1)}, u32[]{:S(2)}, u32[]{:S(2)}) collective-permute-start(bf16[128,64,128]{2,1,0:T(8,128)(2,1)S(1)} %pad_maximum_fusion.refs_0_), channel_id=1, source_target_pairs={{1,0},{0,1},{11,10},{10,11},{21,20},{20,21},{31,30},{30,31}} | collective-permute-start | bytes 6291464 | tf_op jit(solution)/shard_map/ppermute | solution.py:240
  21.4 48.8 %collective-permute-start.5 = (bf16[128,64,128]{2,1,0:T(8,128)(2,1)S(1)}, bf16[128,64,128]{2,1,0:T(8,128)(2,1)S(1)}, u32[]{:S(2)}, u32[]{:S(2)}) collective-permute-start(bf16[128,64,128]{2,1,0:T(8,128)(2,1)S(1)} %pad_maximum_fusion.refs_0_), channel_id=1, source_target_pairs={{17,0},{16,1},{27,10},{26,11},{5,20},{4,21},{15,30},{14,31}} | collective-permute-start | bytes 6291464 | tf_op jit(solution)/shard_map/ppermute | solution.py:240
  60.4 13.1 %copy-start.7 = (bf16[128,32,128]{2,1,0:T(8,128)(2,1)}, bf16[128,32,128]{2,1,0:T(8,128)(2,1)S(1)}, u32[]{:S(2)}) copy-start(bf16[128,32,128]{2,1,0:T(8,128)(2,1)S(1)} %collective-permute-done.2) | copy-start | bytes 3145732
  60.4 11.1 %collective-permute-start.3 = (bf16[128,64,128]{2,1,0:T(8,128)(2,1)}, bf16[128,64,128]{2,1,0:T(8,128)(2,1)}, u32[]{:S(2)}, u32[]{:S(2)}) collective-permute-start(bf16[128,64,128]{2,1,0:T(8,128)(2,1)} %collective-permute-done.1.refs_1_), channel_id=1, source_target_pairs={{2,4},{3,5},{12,14},{13,15},{18,20},{19,21},{28,30},{29,31}} | collective-permute-start | bytes 6291464 | tf_op jit(solution)/shard_map/ppermute | solution.py:240
  62.4 12.3 %collective-permute-start.11 = (bf16[128,32,128]{2,1,0:T(8,128)(2,1)S(1)}, bf16[128,32,128]{2,1,0:T(8,128)(2,1)S(1)}, u32[]{:S(2)}, u32[]{:S(2)}) collective-permute-start(bf16[128,32,128]{2,1,0:T(8,128)(2,1)S(1)} %collective-permute-done.2), channel_id=1, source_target_pairs={{0,8},{1,9},{2,10},{3,11},{4,12},{5,13},{6,14},{7,15},{8,0},{9,1},... | collective-permute-start | bytes 3145736 | tf_op jit(solution)/shard_map/ppermute | solution.py:240
  62.5 28.4 %collective-permute-start.7 = (bf16[128,64,128]{2,1,0:T(8,128)(2,1)}, bf16[128,64,128]{2,1,0:T(8,128)(2,1)}, u32[]{:S(2)}, u32[]{:S(2)}) collective-permute-start(bf16[128,64,128]{2,1,0:T(8,128)(2,1)} %collective-permute-done.1.refs_1_), channel_id=1, source_target_pairs={{18,2},{19,3},{28,12},{29,13},{6,22},{7,23}} | collective-permute-start | bytes 6291464 | tf_op jit(solution)/shard_map/ppermute | solution.py:240
  68.1 3.3 %copy-start.5 = (bf16[128,64,128]{2,1,0:T(8,128)(2,1)}, bf16[128,64,128]{2,1,0:T(8,128)(2,1)S(1)}, u32[]{:S(2)}) copy-start(bf16[128,64,128]{2,1,0:T(8,128)(2,1)S(1)} %collective-permute-done.4.refs_0_) | copy-start | bytes 6291460
  68.2 22.7 %collective-permute-start.8 = (bf16[128,64,128]{2,1,0:T(8,128)(2,1)}, bf16[128,64,128]{2,1,0:T(8,128)(2,1)}, u32[]{:S(2)}, u32[]{:S(2)}) collective-permute-start(bf16[128,64,128]{2,1,0:T(8,128)(2,1)} %collective-permute-done.1.refs_1_), channel_id=1, source_target_pairs={{3,2},{2,3},{13,12},{12,13},{23,22},{22,23}} | collective-permute-start | bytes 6291464 | tf_op jit(solution)/shard_map/ppermute | solution.py:240
  70.1 1.4 copy-start.4
  71.5 19.3 %collective-permute-start.10 = (bf16[128,64,128]{2,1,0:T(8,128)(2,1)}, bf16[128,64,128]{2,1,0:T(8,128)(2,1)}, u32[]{:S(2)}, u32[]{:S(2)}) collective-permute-start(bf16[128,64,128]{2,1,0:T(8,128)(2,1)} %collective-permute-done.3.refs_2_), channel_id=1, source_target_pairs={{5,4},{4,5},{15,14},{14,15}} | collective-permute-start | bytes 6291464 | tf_op jit(solution)/shard_map/ppermute | solution.py:240
  73.5 43.0 %collective-permute-start.6 = (bf16[128,64,128]{2,1,0:T(8,128)(2,1)}, bf16[128,64,128]{2,1,0:T(8,128)(2,1)}, u32[]{:S(2)}, u32[]{:S(2)}) collective-permute-start(bf16[128,64,128]{2,1,0:T(8,128)(2,1)} %collective-permute-done.3.refs_2_), channel_id=1, source_target_pairs={{4,6},{5,7},{20,22},{21,23}} | collective-permute-start | bytes 6291464 | tf_op jit(solution)/shard_map/ppermute | solution.py:240
  74.8 41.7 %collective-permute-start.9 = (bf16[128,64,128]{2,1,0:T(8,128)(2,1)}, bf16[128,64,128]{2,1,0:T(8,128)(2,1)}, u32[]{:S(2)}, u32[]{:S(2)}) collective-permute-start(bf16[128,64,128]{2,1,0:T(8,128)(2,1)} %collective-permute-done.3.refs_2_), channel_id=1, source_target_pairs={{20,4},{21,5},{30,14},{31,15}} | collective-permute-start | bytes 6291464 | tf_op jit(solution)/shard_map/ppermute | solution.py:240
  78.6 9.0 %copy-start.3 = (bf16[128,64,128]{2,1,0:T(8,128)(2,1)}, bf16[128,64,128]{2,1,0:T(8,128)(2,1)S(1)}, u32[]{:S(2)}) copy-start(bf16[128,64,128]{2,1,0:T(8,128)(2,1)S(1)} %pad_maximum_fusion.1.refs_1_.refs_0_) | copy-start | bytes 6291460
  87.5 3.3 %copy-start = (bf16[64,256,256]{2,1,0:T(8,128)(2,1)}, bf16[64,256,256]{2,1,0:T(8,128)(2,1)S(1)}, u32[]{:S(2)}) copy-start(bf16[64,256,256]{2,1,0:T(8,128)(2,1)S(1)} %get-tuple-element.33.refs_4_) | copy-start | bytes 25165828
  116.5 28.1 %collective-permute-start.13 = (bf16[128,64,128]{2,1,0:T(8,128)(2,1)}, bf16[128,64,128]{2,1,0:T(8,128)(2,1)S(1)}, u32[]{:S(2)}, u32[]{:S(2)}) collective-permute-start(bf16[128,64,128]{2,1,0:T(8,128)(2,1)} %collective-permute-done.6.refs_3_), channel_id=1, source_target_pairs={{22,6},{23,7}} | collective-permute-start | bytes 6291464 | tf_op jit(solution)/shard_map/ppermute | solution.py:240
  117.8 34.2 %collective-permute-start.16 = (bf16[128,64,128]{2,1,0:T(8,128)(2,1)}, bf16[128,64,128]{2,1,0:T(8,128)(2,1)}, u32[]{:S(2)}, u32[]{:S(2)}) collective-permute-start(bf16[128,64,128]{2,1,0:T(8,128)(2,1)} %collective-permute-done.6.refs_3_), channel_id=1, source_target_pairs={{7,6},{6,7}} | collective-permute-start | bytes 6291464 | tf_op jit(solution)/shard_map/ppermute | solution.py:240
  122.6 63.1 %collective-permute-start.12 = (bf16[128,64,128]{2,1,0:T(8,128)(2,1)}, bf16[128,64,128]{2,1,0:T(8,128)(2,1)}, u32[]{:S(2)}, u32[]{:S(2)}) collective-permute-start(bf16[128,64,128]{2,1,0:T(8,128)(2,1)} %collective-permute-done.7.refs_1_), channel_id=1, source_target_pairs={{3,2},{2,3},{13,12},{12,13},{23,22},{22,23}} | collective-permute-start | bytes 6291464 | tf_op jit(solution)/shard_map/ppermute | solution.py:240
  144.7 24.1 %copy-start.6 = (bf16[128,64,128]{2,1,0:T(8,128)(2,1)}, bf16[128,64,128]{2,1,0:T(8,128)(2,1)S(1)}, u32[]{:S(2)}) copy-start(bf16[128,64,128]{2,1,0:T(8,128)(2,1)S(1)} %collective-permute-done.13.refs_3_) | copy-start | bytes 6291460
  144.7 41.0 %collective-permute-start.14 = (bf16[128,64,128]{2,1,0:T(8,128)(2,1)}, bf16[128,64,128]{2,1,0:T(8,128)(2,1)}, u32[]{:S(2)}, u32[]{:S(2)}) collective-permute-start(bf16[128,64,128]{2,1,0:T(8,128)(2,1)} %collective-permute-done.3.refs_2_), channel_id=1, source_target_pairs={{21,4},{20,5},{31,14},{30,15}} | collective-permute-start | bytes 6291464 | tf_op jit(solution)/shard_map/ppermute | solution.py:240
  146.6 39.0 %collective-permute-start.15 = (bf16[128,64,128]{2,1,0:T(8,128)(2,1)S(1)}, bf16[128,64,128]{2,1,0:T(8,128)(2,1)}, u32[]{:S(2)}, u32[]{:S(2)}) collective-permute-start(bf16[128,64,128]{2,1,0:T(8,128)(2,1)S(1)} %collective-permute-done.13.refs_3_), channel_id=1, source_target_pairs={{7,6},{6,7}} | collective-permute-start | bytes 6291464 | tf_op jit(solution)/shard_map/ppermute | solution.py:240

commit v4 on v3

--- a/solution.py
+++ b/solution.py
@@ -267,20 +267,20 @@
     after = lax.optimization_barrier
     once = climb(joined, 1)
     side_zero = to_row(joined, 0, 1, 0)
-    both_zero = to_row(joined, 0, 1, 1)
-    once, table, across = after((once, table, across))
+    once, table, across, kept = after((once, table, across, joined))
     twice = climb(once, 2)
     joined_across = join(across, send(across, core_flip))
     offsets = jnp.stack([2 * chip * width, 2 * (1 - chip) * width]).astype(jnp.int32)
     right, out = weights(offsets, [joined, joined_across], sides * rows * width)
     chip_one = to_row(once, 1, 0, 1)
     side_one = to_row(once, 1, 1, 0)
-    twice, side_zero, both_zero = after((twice, side_zero, both_zero))
+    both_zero = to_row(kept, 0, 1, 1)
+    twice, side_zero, side_one = after((twice, side_zero, side_one))
     thrice = climb(twice, 3)
     chip_two = to_row(twice, 2, 0, 1)
     side_two = to_row(twice, 2, 1, 0)
-    thrice, chip_one, side_one, chip_two, side_two, twice, right, out = after(
-        (thrice, chip_one, side_one, chip_two, side_two, twice, right, out)
+    thrice, chip_one, both_zero, chip_two, side_two, twice, right, out = after(
+        (thrice, chip_one, both_zero, chip_two, side_two, twice, right, out)
     )
     both_one = to_row(chip_one, 1, 1, 0)
     chip_three = to_row(thrice, 3, 0, 1)

time: 204 us -> 202 us (level)
  the two profiles are of different devices: /device:TPU:26 before, /device:TPU:20 now
where the time goes in v4:
time: 202 us; the launch traced here: 201 us
  Pallas kernels  82.9 us (41%)
  starting transfers between devices  60.3 us (30%)
  waiting for transfers between devices  40.5 us (20%)
  other arithmetic  9.93 us (5%)
  local copies, waits for them, and re-layouts  6.8 us (3%)
    pallas_call x4, Pallas kernels, pair_block(): pl.pallas_call(functools.partial(pair_kernel, count=count, height=height,...  67 us
    ppermute x17, starting transfers between devices, send(): return lax.ppermute(value, axes, number)  60.3 us
    ppermute x17, waiting for transfers between devices, send(): return lax.ppermute(value, axes, number)  40.5 us
    pallas_call x1, Pallas kernels, weights(): pl.pallas_call(functools.partial(weights_kernel, count=count, step=step),...  8.96 us
    pallas_call x1, Pallas kernels, whiten(): pl.pallas_call(functools.partial(whiten_kernel, width=width, parts=parts)...  6.96 us
    unnamed x16, local copies, waits for them, and re-layouts  6.2 us
  transfers between devices with their start and end apart: 17, of which 7 were waited for; matrix products, arithmetic and copies ran while one was open for 5% of the time, Pallas kernels for 29%

profile of v4, /device:TPU:20, one launch (start us, length us, event | category | flops | bytes accessed | tf_op | source)
XLA Modules:
  0.0 201.5 jit_solution(16037048437378734405)
XLA Ops:
  0.0 1.6 copy-done.1
  1.6 7.0 %whiten.1 = bf16[128,32,128]{2,1,0:T(8,128)(2,1)S(1)} custom-call(f32[1024,512]{1,0:T(8,128)S(1)} %bitcast.12, f32[1024,512]{1,0:T(8,128)S(1)} %bitcast.13, f32[1024,512]{1,0:T(8,128)S(1)} %bitcast.14, f32[1024,512]{1,0:T(8,128)S(1)} %bitcast.15), custom_call_target="tpu_custom_call" | custom-call | tf_op jit(solution)/shard_map/whiten/pallas_call | solution.py:51
  8.6 0.1 collective-permute-start
  8.7 2.6 %collective-permute-done = bf16[128,32,128]{2,1,0:T(8,128)(2,1)S(1)} collective-permute-done((bf16[128,32,128]{2,1,0:T(8,128)(2,1)S(1)}, bf16[128,32,128]{2,1,0:T(8,128)(2,1)S(1)}, u32[]{:S(2)}, u32[]{:S(2)}) %collective-permute-start) | collective-permute-done | bytes 1048608 | tf_op jit(solution)/shard_map/ppermute | solution.py:240
  11.3 0.1 broadcast_select_fusion.3
  11.4 0.0 copy-start.7
  11.4 0.3 pad_maximum_fusion.refs_0_
  11.7 0.0 copy-start.2
  11.7 4.8 %collective-permute-start.1 = (bf16[128,64,128]{2,1,0:T(8,128)(2,1)S(1)}, bf16[128,64,128]{2,1,0:T(8,128)(2,1)}, u32[]{:S(2)}, u32[]{:S(2)}) collective-permute-start(bf16[128,64,128]{2,1,0:T(8,128)(2,1)S(1)} %pad_maximum_fusion.refs_0_), channel_id=1, source_target_pairs={{0,2},{1,3},{4,6},{5,7},{10,12},{11,13},{16,18},{17,19},{20,22},{2... | collective-permute-start | bytes 6291464 | tf_op jit(solution)/shard_map/ppermute | solution.py:240
  16.5 0.5 collective-permute-start.2
  17.0 0.0 copy-done.7
  17.0 0.6 fusion.15
  17.6 1.3 and_convert_fusion
  18.9 1.3 fusion.14
  20.2 2.0 multiply_convert_fusion.1
  22.2 0.8 pad_maximum_fusion.2.refs_5_
  23.0 3.4 %collective-permute-start.4 = (bf16[128,64,128]{2,1,0:T(8,128)(2,1)S(1)}, bf16[128,64,128]{2,1,0:T(8,128)(2,1)S(1)}, u32[]{:S(2)}, u32[]{:S(2)}) collective-permute-start(bf16[128,64,128]{2,1,0:T(8,128)(2,1)S(1)} %pad_maximum_fusion.refs_0_), channel_id=1, source_target_pairs={{1,0},{0,1},{11,10},{10,11},{21,20},{20,21},{31,30},{30,31}} | collective-permute-start | bytes 6291464 | tf_op jit(solution)/shard_map/ppermute | solution.py:240
  26.4 11.9 %collective-permute-done.2 = bf16[128,32,128]{2,1,0:T(8,128)(2,1)S(1)} collective-permute-done((bf16[128,32,128]{2,1,0:T(8,128)(2,1)S(1)}, bf16[128,32,128]{2,1,0:T(8,128)(2,1)S(1)}, u32[]{:S(2)}, u32[]{:S(2)}) %collective-permute-start.2) | collective-permute-done | bytes 1048608 | tf_op jit(solution)/shard_map/ppermute | solution.py:240
  38.3 0.5 collective-permute-done.1.refs_1_
  38.7 1.3 collective-permute-start.3
  40.0 2.0 collective-permute-start.5
  42.0 3.4 %collective-permute-start.11 = (bf16[128,32,128]{2,1,0:T(8,128)(2,1)S(1)}, bf16[128,32,128]{2,1,0:T(8,128)(2,1)S(1)}, u32[]{:S(2)}, u32[]{:S(2)}) collective-permute-start(bf16[128,32,128]{2,1,0:T(8,128)(2,1)S(1)} %collective-permute-done.2), channel_id=1, source_target_pairs={{0,8},{1,9},{2,10},{3,11},{4,12},{5,13},{6,14},{7,15},{8,0},{9,1},... | collective-permute-start | bytes 3145736 | tf_op jit(solution)/shard_map/ppermute | solution.py:240
  45.4 2.0 collective-permute-start.7
  47.4 3.6 %collective-permute-done.4.refs_0_ = bf16[128,64,128]{2,1,0:T(8,128)(2,1)S(1)} collective-permute-done((bf16[128,64,128]{2,1,0:T(8,128)(2,1)S(1)}, bf16[128,64,128]{2,1,0:T(8,128)(2,1)S(1)}, u32[]{:S(2)}, u32[]{:S(2)}) %collective-permute-start.4) | collective-permute-done | bytes 2097184 | tf_op jit(solution)/shard_map/ppermute | solution.py:240
  50.9 1.3 copy-done.4
  52.2 1.3 collective-permute-start.8
  53.5 0.0 copy-done.6
  53.5 13.4 %collective-permute-done.3.refs_2_ = bf16[128,64,128]{2,1,0:T(8,128)(2,1)} collective-permute-done((bf16[128,64,128]{2,1,0:T(8,128)(2,1)}, bf16[128,64,128]{2,1,0:T(8,128)(2,1)}, u32[]{:S(2)}, u32[]{:S(2)}) %collective-permute-start.3) | collective-permute-done | bytes 2097184 | tf_op jit(solution)/shard_map/ppermute | solution.py:240
  67.0 0.0 collective-permute-done.5.refs_1_
  67.0 2.0 %collective-permute-start.10 = (bf16[128,64,128]{2,1,0:T(8,128)(2,1)}, bf16[128,64,128]{2,1,0:T(8,128)(2,1)}, u32[]{:S(2)}, u32[]{:S(2)}) collective-permute-start(bf16[128,64,128]{2,1,0:T(8,128)(2,1)} %collective-permute-done.3.refs_2_), channel_id=1, source_target_pairs={{5,4},{4,5},{15,14},{14,15}} | collective-permute-start | bytes 6291464 | tf_op jit(solution)/shard_map/ppermute | solution.py:240
  69.0 7.9 %collective-permute-start.6 = (bf16[128,64,128]{2,1,0:T(8,128)(2,1)}, bf16[128,64,128]{2,1,0:T(8,128)(2,1)}, u32[]{:S(2)}, u32[]{:S(2)}) collective-permute-start(bf16[128,64,128]{2,1,0:T(8,128)(2,1)} %collective-permute-done.3.refs_2_), channel_id=1, source_target_pairs={{4,6},{5,7},{20,22},{21,23}} | collective-permute-start | bytes 6291464 | tf_op jit(solution)/shard_map/ppermute | solution.py:240
  76.9 0.0 collective-permute-done.11
  76.9 2.6 %collective-permute-start.9 = (bf16[128,64,128]{2,1,0:T(8,128)(2,1)}, bf16[128,64,128]{2,1,0:T(8,128)(2,1)}, u32[]{:S(2)}, u32[]{:S(2)}) collective-permute-start(bf16[128,64,128]{2,1,0:T(8,128)(2,1)} %collective-permute-done.3.refs_2_), channel_id=1, source_target_pairs={{20,4},{21,5},{30,14},{31,15}} | collective-permute-start | bytes 6291464 | tf_op jit(solution)/shard_map/ppermute | solution.py:240
  79.5 0.1 pad_add_fusion.1.offset_ref
  79.6 1.4 broadcast_select_fusion.1
  80.9 0.3 pad_maximum_fusion.1.refs_1_.refs_0_
  81.2 0.0 copy-done.2
  81.3 0.0 copy-start.3
  81.3 9.0 %weights.1 = (bf16[64,256,256]{2,1,0:T(8,128)(2,1)S(1)}, bf16[201,256,128]{2,1,0:T(8,128)(2,1)}) custom-call(s32[2]{0:T(128)S(1)} %pad_add_fusion.1.offset_ref, bf16[128,64,128]{2,1,0:T(8,128)(2,1)S(1)} %pad_maximum_fusion.refs_0_, bf16[128,64,128]{2,1,0:T(8,128)(2,1)S(1)} %pad_maximum_fusion.1.refs_1_.refs_0_), custom_call_target="tpu_custom_call" | custom-call | tf_op jit(solution)/shard_map/weights/pallas_call | solution.py:89
  90.2 0.0 copy-done.3
  90.2 3.3 %copy-done = bf16[64,256,256]{2,1,0:T(8,128)(2,1)} copy-done((bf16[64,256,256]{2,1,0:T(8,128)(2,1)}, bf16[64,256,256]{2,1,0:T(8,128)(2,1)S(1)}, u32[]{:S(2)}) %copy-start) | copy-done | bytes 8388632
  93.5 0.0 collective-permute-done.7.refs_1_
  93.5 0.0 collective-permute-done.8.refs_0_
  93.5 0.0 collective-permute-done.10.refs_2_
  93.5 5.8 %collective-permute-done.6.refs_3_ = bf16[128,64,128]{2,1,0:T(8,128)(2,1)} collective-permute-done((bf16[128,64,128]{2,1,0:T(8,128)(2,1)}, bf16[128,64,128]{2,1,0:T(8,128)(2,1)}, u32[]{:S(2)}, u32[]{:S(2)}) %collective-permute-start.6) | collective-permute-done | bytes 2097184 | tf_op jit(solution)/shard_map/ppermute | solution.py:240
  99.4 2.6 %collective-permute-done.9.refs_2_ = bf16[128,64,128]{2,1,0:T(8,128)(2,1)} collective-permute-done((bf16[128,64,128]{2,1,0:T(8,128)(2,1)}, bf16[128,64,128]{2,1,0:T(8,128)(2,1)}, u32[]{:S(2)}, u32[]{:S(2)}) %collective-permute-start.9) | collective-permute-done | bytes 2097184 | tf_op jit(solution)/shard_map/ppermute | solution.py:240
  102.0 0.8 collective-permute-start.13
  102.8 2.0 collective-permute-start.16
  105.4 0.6 pad_add_fusion.2.meta_ref
  106.0 2.0 %collective-permute-start.12 = (bf16[128,64,128]{2,1,0:T(8,128)(2,1)}, bf16[128,64,128]{2,1,0:T(8,128)(2,1)}, u32[]{:S(2)}, u32[]{:S(2)}) collective-permute-start(bf16[128,64,128]{2,1,0:T(8,128)(2,1)} %collective-permute-done.7.refs_1_), channel_id=1, source_target_pairs={{3,2},{2,3},{13,12},{12,13},{23,22},{22,23}} | collective-permute-start | bytes 6291464 | tf_op jit(solution)/shard_map/ppermute | solution.py:240
  108.0 16.7 %pair_block.4.refs_6_ = bf16[201,256,128]{2,1,0:T(8,128)(2,1)} custom-call(s32[2]{0:T(128)} %pad_add_fusion.2.meta_ref, bf16[128,64,128]{2,1,0:T(8,128)(2,1)} %copy-done.2, bf16[128,64,128]{2,1,0:T(8,128)(2,1)} %collective-permute-done.1.refs_1_, bf16[128,64,128]{2,1,0:T(8,128)(2,1)} %collective-permute-done.3.refs_2_, ...), custom_call_target="tpu_custom_call", output_to_operand_aliasing={{}: (7, {})} | custom-call | flops 7784628224 | bytes 11681792 | tf_op jit(solution)/shard_map/pair_block/pallas_call | solution.py:182
  124.7 0.0 collective-permute-done.13.refs_3_
  124.7 22.4 %collective-permute-start.14 = (bf16[128,64,128]{2,1,0:T(8,128)(2,1)}, bf16[128,64,128]{2,1,0:T(8,128)(2,1)}, u32[]{:S(2)}, u32[]{:S(2)}) collective-permute-start(bf16[128,64,128]{2,1,0:T(8,128)(2,1)} %collective-permute-done.3.refs_2_), channel_id=1, source_target_pairs={{21,4},{20,5},{31,14},{30,15}} | collective-permute-start | bytes 6291464 | tf_op jit(solution)/shard_map/ppermute | solution.py:240
  147.1 2.0 collective-permute-start.15
  149.1 0.7 pad_add_fusion.4.meta_ref
  149.7 0.7 pad_add_fusion.3.meta_ref
  150.4 0.6 pad_add_fusion.meta_ref
  150.9 0.0 collective-permute-done.16.refs_3_
  150.9 16.7 %pair_block.5.refs_6_ = bf16[201,256,128]{2,1,0:T(8,128)(2,1)} custom-call(s32[2]{0:T(128)} %pad_add_fusion.4.meta_ref, bf16[128,64,128]{2,1,0:T(8,128)(2,1)} %copy-done.4, bf16[128,64,128]{2,1,0:T(8,128)(2,1)} %collective-permute-done.5.refs_1_, bf16[128,64,128]{2,1,0:T(8,128)(2,1)} %collective-permute-done.10.refs_2_, ...), custom_call_target="tpu_custom_call", output_to_operand_aliasing={{}: (7, {})} | custom-call | flops 7784628224 | bytes 11681792 | tf_op jit(solution)/shard_map/pair_block/pallas_call | solution.py:182
  167.7 16.9 %pair_block.6.refs_6_ = bf16[201,256,128]{2,1,0:T(8,128)(2,1)} custom-call(s32[2]{0:T(128)} %pad_add_fusion.3.meta_ref, bf16[128,64,128]{2,1,0:T(8,128)(2,1)} %copy-done.3, bf16[128,64,128]{2,1,0:T(8,128)(2,1)} %collective-permute-done.7.refs_1_, bf16[128,64,128]{2,1,0:T(8,128)(2,1)} %collective-permute-done.9.refs_2_, ...), custom_call_target="tpu_custom_call", output_to_operand_aliasing={{}: (7, {})} | custom-call | flops 7784628224 | bytes 11681792 | tf_op jit(solution)/shard_map/pair_block/pallas_call | solution.py:182
  184.6 0.0 collective-permute-done.12.refs_1_
  184.6 0.0 collective-permute-done.14.refs_2_
  184.6 0.0 collective-permute-done.15.refs_3_
  184.6 16.7 %pair_block.7 = bf16[201,256,128]{2,1,0:T(8,128)(2,1)} custom-call(s32[2]{0:T(128)} %pad_add_fusion.meta_ref, bf16[128,64,128]{2,1,0:T(8,128)(2,1)} %collective-permute-done.8.refs_0_, bf16[128,64,128]{2,1,0:T(8,128)(2,1)} %collective-permute-done.12.refs_1_, bf16[128,64,128]{2,1,0:T(8,128)(2,1)} %collective-permute-done.14.refs_2_, ...), custom_call_target="tpu_custom_call", output_to_operand_aliasing={{}: (7, {})} | custom-call | flops 7784628224 | bytes 11681792 | tf_op jit(solution)/shard_map/pair_block/pallas_call | solution.py:182
  (8 shorter events, 0.0 us)
Async XLA Ops:
  0.0 1.6 copy-start.1
  8.6 2.7 %collective-permute-start = (bf16[128,32,128]{2,1,0:T(8,128)(2,1)S(1)}, bf16[128,32,128]{2,1,0:T(8,128)(2,1)S(1)}, u32[]{:S(2)}, u32[]{:S(2)}) collective-permute-start(bf16[128,32,128]{2,1,0:T(8,128)(2,1)S(1)} %whiten.1), channel_id=1, source_target_pairs={{0,8},{1,9},{2,10},{3,11},{4,12},{5,13},{6,14},{7,15},{8,0},{9,1},... | collective-permute-start | bytes 3145736 | tf_op jit(solution)/shard_map/ppermute | solution.py:240
  11.4 5.6 %copy-start.7 = (s32[2]{0:T(128)S(1)}, s32[2]{0:T(128)}, u32[]{:S(2)}) copy-start(s32[2]{0:T(128)} %param.5) | copy-start | bytes 28
  11.7 69.5 %copy-start.2 = (bf16[128,64,128]{2,1,0:T(8,128)(2,1)}, bf16[128,64,128]{2,1,0:T(8,128)(2,1)S(1)}, u32[]{:S(2)}) copy-start(bf16[128,64,128]{2,1,0:T(8,128)(2,1)S(1)} %pad_maximum_fusion.refs_0_) | copy-start | bytes 6291460
  11.7 27.0 %collective-permute-start.1 = (bf16[128,64,128]{2,1,0:T(8,128)(2,1)S(1)}, bf16[128,64,128]{2,1,0:T(8,128)(2,1)}, u32[]{:S(2)}, u32[]{:S(2)}) collective-permute-start(bf16[128,64,128]{2,1,0:T(8,128)(2,1)S(1)} %pad_maximum_fusion.refs_0_), channel_id=1, source_target_pairs={{0,2},{1,3},{4,6},{5,7},{10,12},{11,13},{16,18},{17,19},{20,22},{2... | collective-permute-start | bytes 6291464 | tf_op jit(solution)/shard_map/ppermute | solution.py:240
  16.5 21.8 %collective-permute-start.2 = (bf16[128,32,128]{2,1,0:T(8,128)(2,1)S(1)}, bf16[128,32,128]{2,1,0:T(8,128)(2,1)S(1)}, u32[]{:S(2)}, u32[]{:S(2)}) collective-permute-start(bf16[128,32,128]{2,1,0:T(8,128)(2,1)S(1)} %whiten.1), channel_id=1, source_target_pairs={{0,16},{1,17},{2,18},{3,19},{4,20},{5,21},{6,22},{7,23},{8,24},{9,... | collective-permute-start | bytes 3145736 | tf_op jit(solution)/shard_map/ppermute | solution.py:240
  23.0 27.9 %collective-permute-start.4 = (bf16[128,64,128]{2,1,0:T(8,128)(2,1)S(1)}, bf16[128,64,128]{2,1,0:T(8,128)(2,1)S(1)}, u32[]{:S(2)}, u32[]{:S(2)}) collective-permute-start(bf16[128,64,128]{2,1,0:T(8,128)(2,1)S(1)} %pad_maximum_fusion.refs_0_), channel_id=1, source_target_pairs={{1,0},{0,1},{11,10},{10,11},{21,20},{20,21},{31,30},{30,31}} | collective-permute-start | bytes 6291464 | tf_op jit(solution)/shard_map/ppermute | solution.py:240
  38.3 15.2 %copy-start.6 = (bf16[128,32,128]{2,1,0:T(8,128)(2,1)}, bf16[128,32,128]{2,1,0:T(8,128)(2,1)S(1)}, u32[]{:S(2)}) copy-start(bf16[128,32,128]{2,1,0:T(8,128)(2,1)S(1)} %collective-permute-done.2) | copy-start | bytes 3145732
  38.7 28.2 %collective-permute-start.3 = (bf16[128,64,128]{2,1,0:T(8,128)(2,1)}, bf16[128,64,128]{2,1,0:T(8,128)(2,1)}, u32[]{:S(2)}, u32[]{:S(2)}) collective-permute-start(bf16[128,64,128]{2,1,0:T(8,128)(2,1)} %collective-permute-done.1.refs_1_), channel_id=1, source_target_pairs={{2,4},{3,5},{12,14},{13,15},{18,20},{19,21},{28,30},{29,31}} | collective-permute-start | bytes 6291464 | tf_op jit(solution)/shard_map/ppermute | solution.py:240
  40.0 26.9 %collective-permute-start.5 = (bf16[128,64,128]{2,1,0:T(8,128)(2,1)}, bf16[128,64,128]{2,1,0:T(8,128)(2,1)}, u32[]{:S(2)}, u32[]{:S(2)}) collective-permute-start(bf16[128,64,128]{2,1,0:T(8,128)(2,1)} %collective-permute-done.1.refs_1_), channel_id=1, source_target_pairs={{3,2},{2,3},{13,12},{12,13},{23,22},{22,23}} | collective-permute-start | bytes 6291464 | tf_op jit(solution)/shard_map/ppermute | solution.py:240
  42.0 34.8 %collective-permute-start.11 = (bf16[128,32,128]{2,1,0:T(8,128)(2,1)S(1)}, bf16[128,32,128]{2,1,0:T(8,128)(2,1)S(1)}, u32[]{:S(2)}, u32[]{:S(2)}) collective-permute-start(bf16[128,32,128]{2,1,0:T(8,128)(2,1)S(1)} %collective-permute-done.2), channel_id=1, source_target_pairs={{0,8},{1,9},{2,10},{3,11},{4,12},{5,13},{6,14},{7,15},{8,0},{9,1},... | collective-permute-start | bytes 3145736 | tf_op jit(solution)/shard_map/ppermute | solution.py:240
  45.4 48.1 %collective-permute-start.7 = (bf16[128,64,128]{2,1,0:T(8,128)(2,1)}, bf16[128,64,128]{2,1,0:T(8,128)(2,1)}, u32[]{:S(2)}, u32[]{:S(2)}) collective-permute-start(bf16[128,64,128]{2,1,0:T(8,128)(2,1)} %collective-permute-done.1.refs_1_), channel_id=1, source_target_pairs={{18,2},{19,3},{28,12},{29,13},{6,22},{7,23}} | collective-permute-start | bytes 6291464 | tf_op jit(solution)/shard_map/ppermute | solution.py:240
  50.9 1.3 copy-start.4
  52.2 41.3 %collective-permute-start.8 = (bf16[128,64,128]{2,1,0:T(8,128)(2,1)S(1)}, bf16[128,64,128]{2,1,0:T(8,128)(2,1)}, u32[]{:S(2)}, u32[]{:S(2)}) collective-permute-start(bf16[128,64,128]{2,1,0:T(8,128)(2,1)S(1)} %pad_maximum_fusion.refs_0_), channel_id=1, source_target_pairs={{17,0},{16,1},{27,10},{26,11},{5,20},{4,21},{15,30},{14,31}} | collective-permute-start | bytes 6291464 | tf_op jit(solution)/shard_map/ppermute | solution.py:240
  67.0 26.5 %collective-permute-start.10 = (bf16[128,64,128]{2,1,0:T(8,128)(2,1)}, bf16[128,64,128]{2,1,0:T(8,128)(2,1)}, u32[]{:S(2)}, u32[]{:S(2)}) collective-permute-start(bf16[128,64,128]{2,1,0:T(8,128)(2,1)} %collective-permute-done.3.refs_2_), channel_id=1, source_target_pairs={{5,4},{4,5},{15,14},{14,15}} | collective-permute-start | bytes 6291464 | tf_op jit(solution)/shard_map/ppermute | solution.py:240
  69.0 30.4 %collective-permute-start.6 = (bf16[128,64,128]{2,1,0:T(8,128)(2,1)}, bf16[128,64,128]{2,1,0:T(8,128)(2,1)}, u32[]{:S(2)}, u32[]{:S(2)}) collective-permute-start(bf16[128,64,128]{2,1,0:T(8,128)(2,1)} %collective-permute-done.3.refs_2_), channel_id=1, source_target_pairs={{4,6},{5,7},{20,22},{21,23}} | collective-permute-start | bytes 6291464 | tf_op jit(solution)/shard_map/ppermute | solution.py:240
  76.9 25.1 %collective-permute-start.9 = (bf16[128,64,128]{2,1,0:T(8,128)(2,1)}, bf16[128,64,128]{2,1,0:T(8,128)(2,1)}, u32[]{:S(2)}, u32[]{:S(2)}) collective-permute-start(bf16[128,64,128]{2,1,0:T(8,128)(2,1)} %collective-permute-done.3.refs_2_), channel_id=1, source_target_pairs={{20,4},{21,5},{30,14},{31,15}} | collective-permute-start | bytes 6291464 | tf_op jit(solution)/shard_map/ppermute | solution.py:240
  81.3 9.0 %copy-start.3 = (bf16[128,64,128]{2,1,0:T(8,128)(2,1)}, bf16[128,64,128]{2,1,0:T(8,128)(2,1)S(1)}, u32[]{:S(2)}) copy-start(bf16[128,64,128]{2,1,0:T(8,128)(2,1)S(1)} %pad_maximum_fusion.1.refs_1_.refs_0_) | copy-start | bytes 6291460
  90.2 3.3 %copy-start = (bf16[64,256,256]{2,1,0:T(8,128)(2,1)}, bf16[64,256,256]{2,1,0:T(8,128)(2,1)S(1)}, u32[]{:S(2)}) copy-start(bf16[64,256,256]{2,1,0:T(8,128)(2,1)S(1)} %get-tuple-element.35.refs_4_) | copy-start | bytes 25165828
  102.0 22.7 %collective-permute-start.13 = (bf16[128,64,128]{2,1,0:T(8,128)(2,1)}, bf16[128,64,128]{2,1,0:T(8,128)(2,1)S(1)}, u32[]{:S(2)}, u32[]{:S(2)}) collective-permute-start(bf16[128,64,128]{2,1,0:T(8,128)(2,1)} %collective-permute-done.6.refs_3_), channel_id=1, source_target_pairs={{22,6},{23,7}} | collective-permute-start | bytes 6291464 | tf_op jit(solution)/shard_map/ppermute | solution.py:240
  102.8 48.2 %collective-permute-start.16 = (bf16[128,64,128]{2,1,0:T(8,128)(2,1)}, bf16[128,64,128]{2,1,0:T(8,128)(2,1)}, u32[]{:S(2)}, u32[]{:S(2)}) collective-permute-start(bf16[128,64,128]{2,1,0:T(8,128)(2,1)} %collective-permute-done.6.refs_3_), channel_id=1, source_target_pairs={{7,6},{6,7}} | collective-permute-start | bytes 6291464 | tf_op jit(solution)/shard_map/ppermute | solution.py:240
  106.0 78.6 %collective-permute-start.12 = (bf16[128,64,128]{2,1,0:T(8,128)(2,1)}, bf16[128,64,128]{2,1,0:T(8,128)(2,1)}, u32[]{:S(2)}, u32[]{:S(2)}) collective-permute-start(bf16[128,64,128]{2,1,0:T(8,128)(2,1)} %collective-permute-done.7.refs_1_), channel_id=1, source_target_pairs={{3,2},{2,3},{13,12},{12,13},{23,22},{22,23}} | collective-permute-start | bytes 6291464 | tf_op jit(solution)/shard_map/ppermute | solution.py:240
  124.7 42.9 %copy-start.5 = (bf16[128,64,128]{2,1,0:T(8,128)(2,1)}, bf16[128,64,128]{2,1,0:T(8,128)(2,1)S(1)}, u32[]{:S(2)}) copy-start(bf16[128,64,128]{2,1,0:T(8,128)(2,1)S(1)} %collective-permute-done.13.refs_3_) | copy-start | bytes 6291460
  124.7 59.8 %collective-permute-start.14 = (bf16[128,64,128]{2,1,0:T(8,128)(2,1)}, bf16[128,64,128]{2,1,0:T(8,128)(2,1)}, u32[]{:S(2)}, u32[]{:S(2)}) collective-permute-start(bf16[128,64,128]{2,1,0:T(8,128)(2,1)} %collective-permute-done.3.refs_2_), channel_id=1, source_target_pairs={{21,4},{20,5},{31,14},{30,15}} | collective-permute-start | bytes 6291464 | tf_op jit(solution)/shard_map/ppermute | solution.py:240
  147.1 37.5 %collective-permute-start.15 = (bf16[128,64,128]{2,1,0:T(8,128)(2,1)S(1)}, bf16[128,64,128]{2,1,0:T(8,128)(2,1)}, u32[]{:S(2)}, u32[]{:S(2)}) collective-permute-start(bf16[128,64,128]{2,1,0:T(8,128)(2,1)S(1)} %collective-permute-done.13.refs_3_), channel_id=1, source_target_pairs={{7,6},{6,7}} | collective-permute-start | bytes 6291464 | tf_op jit(solution)/shard_map/ppermute | solution.py:240
